TPU v7x, 512 devices: a whole 4x4x16 slice. The times are simulated.
512 devices in a mesh: cell: 128 (over z, x, core), lag: 4 (over y).
Axes of the slice: x: 4, y: 4, z: 16, core: 2. Of those that a mesh axis runs over, the one named last changes fastest.
Arguments:
- green: bfloat16 [32, 640, 32768], P('lag', None, 'cell'), may hold values from -0.0078125 to 0.0078125
- source: bfloat16 [8, 48, 32768], P(None, None, 'cell'), may hold values from -6 to 6
- observed: float32 [8, 48, 640], replicated, may hold values from -6 to 6
- lag_gaps: int32 [31], replicated, may hold values from 1 to 2, 47 in all
- huber_level: int32 [640], replicated, may hold values from 0 to 7
Outputs:
- gradient: float32 [8, 48, 32768], P(None, 'lag', 'cell')
Inputs may be any that keep to these rules, and one draw needn't show every extreme that they name: `lag_gaps`: the gaps sum to 47.
All inputs are finite; a program needn't handle non-finite values.
Results may differ from a plain program's by a relative error of at most 0.0034.
Values may be sent and summed in bfloat16 or wider, within the bound.
No kernel may reach another device: no remote copies, remote signals or barrier semaphores. Data moves between devices by JAX's collectives and lax.ppermute only.
A program may use at most 64 MiB of HBM per device.

v0:
```python
import jax
import jax.numpy as jnp
from jax import lax
from jax.sharding import PartitionSpec as P


def body(green, source, observed, lag_gaps, huber_level):
    rows, steps, cells = source.shape
    sensors = green.shape[1]
    own_count = green.shape[0]
    lag_table = jnp.concatenate([jnp.zeros((1,), jnp.int32), jnp.cumsum(lag_gaps)])
    first = lax.axis_index("lag") * own_count
    lag_of = lax.dynamic_slice_in_dim(lag_table, first, own_count, 0)
    padded = jnp.concatenate([jnp.zeros_like(source), source], axis=1)
    predicted = jnp.zeros((rows, steps, sensors), jnp.float32)
    for block in range(own_count):
        shifted = lax.dynamic_slice_in_dim(padded, steps - lag_of[block], steps, 1)
        predicted = predicted + jnp.einsum(
            "rtc,sc->rts", shifted, green[block], preferred_element_type=jnp.float32
        )
    threshold = 0.3 * (huber_level.astype(jnp.float32) + 1.0)
    summed = lax.psum(predicted, ("cell", "lag"))
    misfit = summed - observed
    weighted = (misfit * threshold / jnp.maximum(jnp.abs(misfit), threshold)).astype(jnp.bfloat16)
    later = jnp.concatenate([weighted, jnp.zeros_like(weighted)], axis=1)
    terms = jnp.zeros((rows, steps, cells), jnp.float32)
    for block in range(own_count):
        window = lax.dynamic_slice_in_dim(later, lag_of[block], steps, 1)
        terms = terms + jnp.einsum(
            "rts,sc->rtc", window, green[block], preferred_element_type=jnp.float32
        )
    return lax.psum_scatter(terms, "lag", scatter_dimension=1, tiled=True)


def solution(mesh):
    in_specs = (P("lag", None, "cell"), P(None, None, "cell"), P(), P(), P())
    out_specs = P(None, "lag", "cell")
    return jax.shard_map(body, mesh=mesh, in_specs=in_specs, out_specs=out_specs, check_vma=False)
```

profile of v0, /device:TPU:1, one launch (start us, length us, event | category | flops | bytes accessed | tf_op | source)
XLA Modules:
  0.0 550.2 jit_solution(6812498945430603760)
XLA Ops:
  6.5 0.0 copy-start.1
  6.5 0.0 copy-start
  6.5 0.0 all-reduce.4.cloned.1.call-start
  6.5 0.9 copy.10
  7.4 0.1 reduce-window.9
  7.5 0.1 reduce
  7.6 0.1 pad_add_fusion
  7.7 0.1 dynamic_slice.51
  7.8 0.7 fusion.66
  18.6 1.4 fusion.16
  20.0 2.4 convolution_add_fusion.6
  22.5 0.0 copy-done.1
  22.5 0.0 copy-done
  22.5 2.5 convolution_add_fusion.5
  25.0 2.5 convolution_add_fusion.4
  27.6 2.5 convolution_add_fusion.3
  30.1 2.5 convolution_add_fusion.2
  32.7 0.0 copy-start.2
  32.7 2.6 convolution_add_fusion.1
  35.2 2.5 convolution_add_fusion
  37.8 0.0 all-reduce.4.cloned.1.call-update
  37.8 0.0 reduce-scatter.2.cloned.1.call-start
  53.0 0.0 copy-done.2
  53.0 462.0 %all-reduce.4.cloned.1.call-done = f32[8,48,640]{2,1,0:T(8,128)} async-done(((f32[8,48,640]{2,1,0:T(8,128)}), f32[8,48,640]{2,1,0:T(8,128)}) %all-reduce.4.cloned.1.call-update) | async-done | bytes 983056 | tf_op jit(solution)/shard_map/psum | solution.py:22
  515.0 1.7 divide_convert_fusion
  516.7 0.3 fusion
  517.1 0.3 convolution_add_fusion.13
  517.4 0.3 convolution_add_fusion.12
  517.8 0.3 convolution_add_fusion.11
  518.1 0.3 convolution_add_fusion.10
  518.5 0.3 convolution_add_fusion.9
  518.8 0.3 convolution_add_fusion.8
  519.2 0.3 convolution_add_fusion.7
  519.5 1.0 copy.11
  520.5 0.0 reduce-scatter.2.cloned.1.call-update
  520.5 22.9 %reduce-scatter.2.cloned.1.call-done = f32[8,12,256]{2,0,1:T(8,128)} async-done(((f32[8,48,256]{2,0,1:T(8,128)}), f32[8,12,256]{2,0,1:T(8,128)}) %reduce-scatter.2.cloned.1.call-update) | async-done | bytes 98320 | tf_op jit(solution)/shard_map/reduce_scatter | solution.py:32
  (1 shorter events, 0.0 us)
Async XLA Ops:
  6.5 15.9 %copy-start.1 = (bf16[8,640,256]{2,1,0:T(8,128)(2,1)S(1)}, bf16[8,640,256]{2,1,0:T(8,128)(2,1)}, u32[]{:S(2)}) copy-start(bf16[8,640,256]{2,1,0:T(8,128)(2,1)} %param.5) | copy-start | bytes 7864324
  6.5 15.9 %copy-start = (bf16[8,48,256]{2,1,0:T(8,128)(2,1)S(1)}, bf16[8,48,256]{2,1,0:T(8,128)(2,1)}, u32[]{:S(2)}) copy-start(bf16[8,48,256]{2,1,0:T(8,128)(2,1)} %param.6) | copy-start | bytes 589828
  6.5 508.4 %all-reduce.4.cloned.1.call-start = ((), (), s32[]{:S(2)}) async-start(), calls=%async_computation.1 | async-start | bytes 1966080 | tf_op jit(solution)/shard_map/psum | solution.py:22
  32.7 20.3 %copy-start.2 = (s32[640]{0:T(1024)S(1)}, s32[640]{0:T(1024)}, u32[]{:S(2)}) copy-start(s32[640]{0:T(1024)} %param.9) | copy-start | bytes 7684
  37.8 505.6 %reduce-scatter.2.cloned.1.call-start = ((), (), s32[]{:S(2)}) async-start(), calls=%async_computation.2 | async-start | bytes 491520 | tf_op jit(solution)/shard_map/reduce_scatter | solution.py:32
Sparse Core Ops, SparseCore 0:
  37.9 477.0 all-reduce.3
  520.6 22.7 reduce-scatter.1
where the time goes:
time: 553 us; the launch traced here: 550 us
  waiting for transfers between devices  485 us (88%)
  between operations  38.8 us (7%)
  matrix products  21.9 us (4%)
    psum x1, waiting for transfers between devices, body(): summed = lax.psum(predicted, ('cell', 'lag'))  462 us
    reduce_scatter x1, waiting for transfers between devices, body(): return lax.psum_scatter(terms, 'lag', scatter_dimension=1, tiled=True)  22.9 us
    dot_general x8, matrix products, body(): jnp.einsum('rtc,sc->rts', shifted, green[block], preferred_element_type=j...  19.1 us
  transfers between devices with their start and end apart: 2, of which 2 were waited for; matrix products, arithmetic and copies ran while one was open for 0% of the time, Pallas kernels for 0%

commit v1 on v0

v1 whole, which is shorter than its diff:
```python
import jax
import jax.numpy as jnp
from jax import lax
from jax.experimental import pallas as pl
from jax.experimental.pallas import tpu as pltpu
from jax.sharding import Mesh, PartitionSpec as P

PLANE = ("x", "c", "y")
WIRE = jnp.float32
INTERPRET = False


def first_lag(place_ref, gaps_ref, own_count):
    before = place_ref[0] * own_count

    def add(i, total):
        return total + jnp.where(i < before, gaps_ref[i], 0)

    return lax.fori_loop(0, gaps_ref.shape[0], add, jnp.int32(0))


def next_lag(place_ref, gaps_ref, lag, block, own_count):
    at = jnp.minimum(place_ref[0] * own_count + block, gaps_ref.shape[0] - 1)
    return lag + gaps_ref[at]


def forward_kernel(place_ref, gaps_ref, source_ref, green_ref, out_ref, early, total, stage, lag_ref):
    block, blocks = pl.program_id(0), pl.num_programs(0)
    rows, steps, _ = source_ref.shape
    height = rows * steps

    @pl.when(block == 0)
    def _():
        lag_ref[0] = first_lag(place_ref, gaps_ref, blocks)
        total[...] = jnp.zeros_like(total)
        for i in range(early.shape[0]):
            lane = early.shape[2]
            early[i, pl.ds(0, height), :] = jnp.zeros((height, lane), early.dtype)
            for r in range(rows):
                piece = source_ref[r, :, i * lane:(i + 1) * lane].astype(jnp.float32)
                early[i, pl.ds(height + r, steps, stride=rows), :] = piece

    lag = lag_ref[0]
    start = pl.multiple_of((steps - lag) * rows, rows)
    shifted = [early[i, pl.ds(start, height), :].astype(jnp.bfloat16) for i in range(early.shape[0])]
    shifted = jnp.concatenate(shifted, axis=1)
    total[...] += lax.dot_general(
        shifted, green_ref[0], (((1,), (1,)), ((), ())), preferred_element_type=jnp.float32
    )
    lag_ref[0] = next_lag(place_ref, gaps_ref, lag, block, blocks)

    @pl.when(block == blocks - 1)
    def _():
        owners, kept, lanes = out_ref.shape
        part = height // owners
        stage[...] = jnp.zeros_like(stage)
        for q in range(owners):
            for j in range(total.shape[1] // lanes):
                stage[pl.ds(j * part, part), :] = total[pl.ds(q * part, part), pl.ds(j * lanes, lanes)]
            out_ref[q] = stage[...].astype(out_ref.dtype)


def forward(place, gaps, source, green, owners, kept):
    rows, steps, cells = source.shape
    blocks, sensors, _ = green.shape
    height = rows * steps
    return pl.pallas_call(
        forward_kernel,
        grid_spec=pltpu.PrefetchScalarGridSpec(
            num_scalar_prefetch=2,
            grid=(blocks,),
            in_specs=[
                pl.BlockSpec((rows, steps, cells), lambda k, *_: (0, 0, 0)),
                pl.BlockSpec((1, sensors, cells), lambda k, *_: (k, 0, 0)),
            ],
            out_specs=pl.BlockSpec((owners, kept, 128), lambda k, *_: (0, 0, 0)),
            scratch_shapes=[
                pltpu.VMEM((pl.cdiv(cells, 128), 2 * height, min(cells, 128)), jnp.float32),
                pltpu.VMEM((height, sensors), jnp.float32),
                pltpu.VMEM((kept, 128), jnp.float32),
                pltpu.SMEM((1,), jnp.int32),
            ],
        ),
        out_shape=jax.ShapeDtypeStruct((owners, kept, 128), WIRE),
        interpret=INTERPRET,
        name="forward",
    )(place, gaps, source, green)


def adjoint_kernel(place_ref, gaps_ref, weighted_ref, green_ref, out_ref, late, lag_ref):
    block, blocks = pl.program_id(0), pl.num_programs(0)
    owners, _, lanes = weighted_ref.shape
    height = out_ref.shape[0]
    part = height // owners

    @pl.when(block == 0)
    def _():
        lag_ref[0] = first_lag(place_ref, gaps_ref, blocks)
        out_ref[...] = jnp.zeros_like(out_ref)
        late[pl.ds(height, height), :] = jnp.zeros((height, late.shape[1]), late.dtype)
        for q in range(owners):
            piece = weighted_ref[q].astype(jnp.float32)
            for j in range(late.shape[1] // lanes):
                late[pl.ds(q * part, part), pl.ds(j * lanes, lanes)] = piece[j * part:(j + 1) * part]

    lag = lag_ref[0]
    rows = height // 48
    start = pl.multiple_of(lag * rows, rows)
    window = late[pl.ds(start, height), :].astype(jnp.bfloat16)
    out_ref[...] += jnp.dot(window, green_ref[0], preferred_element_type=jnp.float32)
    lag_ref[0] = next_lag(place_ref, gaps_ref, lag, block, blocks)


def adjoint(place, gaps, weighted, green, height):
    blocks, sensors, cells = green.shape
    owners, kept, lanes = weighted.shape
    return pl.pallas_call(
        adjoint_kernel,
        grid_spec=pltpu.PrefetchScalarGridSpec(
            num_scalar_prefetch=2,
            grid=(blocks,),
            in_specs=[
                pl.BlockSpec((owners, kept, lanes), lambda k, *_: (0, 0, 0)),
                pl.BlockSpec((1, sensors, cells), lambda k, *_: (k, 0, 0)),
            ],
            out_specs=pl.BlockSpec((height, cells), lambda k, *_: (0, 0)),
            scratch_shapes=[
                pltpu.VMEM((2 * height, sensors), jnp.float32),
                pltpu.SMEM((1,), jnp.int32),
            ],
        ),
        out_shape=jax.ShapeDtypeStruct((height, cells), jnp.float32),
        interpret=INTERPRET,
        name="adjoint",
    )(place, gaps, weighted, green)


def body(green, source, observed, lag_gaps, huber_level):
    rows, steps, cells = source.shape
    sensors = green.shape[1]
    depth, owners, groups = lax.axis_size("z"), lax.axis_size(PLANE), lax.axis_size("y")
    kept = depth * 4
    part = rows * steps // owners
    place = lax.axis_index("y")[None]

    sent = forward(place, lag_gaps, source, green, owners, kept)
    sent = lax.all_to_all(sent, PLANE, 0, 0, tiled=True)
    plane_sum = jnp.sum(sent.astype(jnp.float32), axis=0).reshape(depth, 4, 128)
    summed = jnp.sum(lax.all_to_all(plane_sum, "z", 0, 0, tiled=True), axis=0)

    p = jnp.minimum(lax.axis_index("z"), depth - 2)
    j, h = p // 3, p % 3
    row = lax.axis_index(PLANE) * part + 4 * h
    seen = lax.dynamic_slice(observed, (row % rows, row // rows, 128 * j), (4, 1, 128)).reshape(4, 128)
    level = lax.dynamic_slice(huber_level, (128 * j,), (128,))
    threshold = 0.3 * (level.astype(jnp.float32) + 1.0)[None]
    misfit = summed - seen
    own = (misfit * threshold / jnp.maximum(jnp.abs(misfit), threshold)).astype(jnp.bfloat16)

    own = lax.all_to_all(jnp.broadcast_to(own[None], (depth, 4, 128)), "z", 0, 0, tiled=True)
    own = jnp.broadcast_to(own.reshape(1, kept, 128), (owners, kept, 128))
    weighted = lax.all_to_all(own, PLANE, 0, 0, tiled=True)

    terms = adjoint(place, lag_gaps, weighted, green, rows * steps)
    terms = terms.reshape(groups, steps // groups, rows, cells)
    terms = jnp.sum(lax.all_to_all(terms, "y", 0, 0, tiled=True), axis=0)
    return terms.transpose(1, 0, 2)


def solution(mesh):
    fine = Mesh(mesh.devices.reshape(16, 4, 2, 4), ("z", "x", "c", "y"))
    cell = ("z", "x", "c")
    in_specs = (P("y", None, cell), P(None, None, cell), P(), P(), P())
    out_specs = P(None, "y", cell)
    return jax.shard_map(body, mesh=fine, in_specs=in_specs, out_specs=out_specs, check_vma=False)
```

time: 553 us -> 111 us (0.20)
  waiting for transfers between devices: 485 us -> 9.89 us
  blocking collectives: 0 us -> 69.3 us
  between operations: 38.8 us -> 0.1 us
  matrix products: 21.9 us -> 0 us
  Pallas kernels: 0 us -> 15.3 us
  starting transfers between devices: 0.04 us -> 13 us
    psum x1 -> x0, waiting for transfers between devices: 462 us -> none  [body(): summed = lax.psum(predicted, ('cell', 'lag'))]
    all_to_all x0 -> x4, blocking collectives: none -> 69.3 us  [the longest x1 26.8 us: body(): sent = lax.all_to_all(sent, PLANE, 0, 0, tiled=True)]
    reduce_scatter x1 -> x0, waiting for transfers between devices: 22.9 us -> none  [body(): return lax.psum_scatter(terms, 'lag', scatter_dimension=1, tiled=True)]
    dot_general x16 -> x0, matrix products: 21.9 us -> none  [the longest x8 19.1 us: body(): jnp.einsum('rtc,sc->rts', shifted, green[block], preferred_element_type=j...]
    pallas_call x0 -> x2, Pallas kernels: none -> 15.3 us  [the longest x1 7.85 us: forward(): pl.pallas_call(forward_kernel, grid_spec=pltpu.PrefetchScalarGridSpec(num...]
    all_to_all x0 -> x1, starting transfers between devices: none -> 13 us  [body(): summed = jnp.sum(lax.all_to_all(plane_sum, 'z', 0, 0, tiled=True), axis=0)]
    all_to_all x0 -> x1, waiting for transfers between devices: none -> 9.89 us  [body(): summed = jnp.sum(lax.all_to_all(plane_sum, 'z', 0, 0, tiled=True), axis=0)]
  transfers between devices with their start and end apart: 2 -> 1, of which waited for: 2 -> 1; matrix products, arithmetic and copies ran while one was open for 0% -> 1% of each run, Pallas kernels for 0% -> 0%
where the time goes in v1:
time: 111 us
  blocking collectives  69.3 us (62%)
  Pallas kernels  15.3 us (14%)
  starting transfers between devices  13 us (12%)
  waiting for transfers between devices  9.89 us (9%)
  other arithmetic  2.15 us (2%)
    all_to_all x1, blocking collectives, body(): sent = lax.all_to_all(sent, PLANE, 0, 0, tiled=True)  26.8 us
    all_to_all x1, blocking collectives, body(): weighted = lax.all_to_all(own, PLANE, 0, 0, tiled=True)  18.1 us
    all_to_all x1, blocking collectives, body(): lax.all_to_all(jnp.broadcast_to(own[None], (depth, 4, 128)), 'z', 0, 0, t...  13.8 us
    all_to_all x1, starting transfers between devices, body(): summed = jnp.sum(lax.all_to_all(plane_sum, 'z', 0, 0, tiled=True), axis=0)  13 us
    all_to_all x1, blocking collectives, body(): terms = jnp.sum(lax.all_to_all(terms, 'y', 0, 0, tiled=True), axis=0)  10.6 us
    all_to_all x1, waiting for transfers between devices, body(): summed = jnp.sum(lax.all_to_all(plane_sum, 'z', 0, 0, tiled=True), axis=0)  9.89 us
    pallas_call x1, Pallas kernels, forward(): pl.pallas_call(forward_kernel, grid_spec=pltpu.PrefetchScalarGridSpec(num...  7.85 us
    pallas_call x1, Pallas kernels, adjoint(): pl.pallas_call(adjoint_kernel, grid_spec=pltpu.PrefetchScalarGridSpec(num...  7.41 us
  transfers between devices with their start and end apart: 1, of which 1 were waited for; matrix products, arithmetic and copies ran while one was open for 1% of the time, Pallas kernels for 0%

profile of v1, /device:TPU:1, one launch (start us, length us, event | category | flops | bytes accessed | tf_op | source)
XLA Modules:
  0.0 110.6 jit_solution(10550578126155277306)
XLA Ops:
  0.0 7.9 %forward.1 = f32[32,64,128]{2,1,0:T(8,128)} custom-call(s32[1]{0:T(128)} %bitcast.place_ref, s32[31]{0:T(128)} %gaps_ref.3, bf16[8,48,256]{2,1,0:T(8,128)(2,1)} %source_ref.1, bf16[8,640,256]{2,1,0:T(8,128)(2,1)} %green_ref.3), custom_call_target="tpu_custom_call" | custom-call | tf_op jit(solution)/shard_map/forward/pallas_call | solution.py:67
  7.9 26.8 %all_to_all.25 = f32[32,64,128]{2,1,0:T(8,128)S(1)} all-to-all(f32[32,64,128]{2,1,0:T(8,128)} %forward.1), channel_id=1, replica_groups=mesh['z'=16,'x'=4,'c'=2,'y'=4] {'x','c','y'}, dimensions={0} | all-to-all | bytes 2097152 | tf_op jit(solution)/shard_map/all_to_all | solution.py:147
  34.6 0.7 reduce_sum.27
  35.3 13.0 %all-to-all-start.1 = ((f32[16,4,128]{2,1,0:T(4,128)}), f32[16,4,128]{2,1,0:T(4,128)S(1)}, u32[]{:S(2)}, u32[]{:S(2)}) async-start(f32[16,4,128]{2,1,0:T(4,128)} %bitcast.1), calls=%async_computation.1 | async-start | bytes 65536 | tf_op jit(solution)/shard_map/all_to_all | solution.py:149
  48.4 0.8 dynamic_slice.6
  49.2 0.8 add_multiply_fusion
  49.9 9.9 %all-to-all-done.1 = f32[16,4,128]{2,1,0:T(4,128)S(1)} async-done(((f32[16,4,128]{2,1,0:T(4,128)}), f32[16,4,128]{2,1,0:T(4,128)S(1)}, u32[]{:S(2)}, u32[]{:S(2)}) %all-to-all-start.1) | async-done | bytes 32800 | tf_op jit(solution)/shard_map/all_to_all | solution.py:149
  59.9 13.8 %all_to_all.26 = bf16[16,4,128]{2,1,0:T(4,128)(2,1)S(1)} all-to-all(bf16[16,4,128]{2,1,0:T(4,128)(2,1)S(1)} %broadcast_in_dim.18), channel_id=1, replica_groups=mesh['z'=16,'x'=4,'c'=2,'y'=4] {'z'}, dimensions={0} | all-to-all | bytes 32768 | tf_op jit(solution)/shard_map/all_to_all | solution.py:160
  73.7 0.1 broadcast_in_dim.20
  73.8 18.1 %all_to_all.27.weighted_ref = bf16[32,64,128]{2,1,0:T(8,128)(2,1)} all-to-all(bf16[32,64,128]{2,1,0:T(8,128)(2,1)S(1)} %broadcast_in_dim.20), channel_id=1, replica_groups=mesh['z'=16,'x'=4,'c'=2,'y'=4] {'x','c','y'}, dimensions={0} | all-to-all | bytes 1048576 | tf_op jit(solution)/shard_map/all_to_all | solution.py:162
  91.9 7.4 %adjoint.1 = f32[384,256]{1,0:T(8,128)} custom-call(s32[1]{0:T(128)} %bitcast.place_ref, s32[31]{0:T(128)} %gaps_ref.3, bf16[32,64,128]{2,1,0:T(8,128)(2,1)} %all_to_all.27.weighted_ref, bf16[8,640,256]{2,1,0:T(8,128)(2,1)} %green_ref.3), custom_call_target="tpu_custom_call" | custom-call | tf_op jit(solution)/shard_map/adjoint/pallas_call | solution.py:117
  99.3 10.6 %all_to_all.28 = f32[4,12,8,256]{3,2,1,0:T(8,128)S(1)} all-to-all(f32[4,12,8,256]{3,2,1,0:T(8,128)} %bitcast.6), channel_id=1, replica_groups=mesh['z'=16,'x'=4,'c'=2,'y'=4] {'y'}, dimensions={0} | all-to-all | bytes 786432 | tf_op jit(solution)/shard_map/all_to_all | solution.py:166
  109.9 0.7 reduce_sum.29
  (3 shorter events, 0.0 us)
Async XLA Ops:
  35.3 24.5 %all-to-all-start.1 = ((f32[16,4,128]{2,1,0:T(4,128)}), f32[16,4,128]{2,1,0:T(4,128)S(1)}, u32[]{:S(2)}, u32[]{:S(2)}) async-start(f32[16,4,128]{2,1,0:T(4,128)} %bitcast.1), calls=%async_computation.1 | async-start | bytes 65536 | tf_op jit(solution)/shard_map/all_to_all | solution.py:149

commit v2 on v0

v2 whole, which is shorter than its diff:
```python
import functools

import jax
import jax.numpy as jnp
from jax import lax
from jax.experimental import pallas as pl
from jax.experimental.pallas import tpu as pltpu
from jax.sharding import Mesh, PartitionSpec as P

PLANE = ("x", "c", "y")
TALL, WIDE = 64, 128
WIRE = jnp.bfloat16
VMEM = pl.BlockSpec(memory_space=pltpu.VMEM)
SMEM = pl.BlockSpec(memory_space=pltpu.SMEM)
LIMIT = pltpu.CompilerParams(vmem_limit_bytes=20 << 20)


def lags(place_ref, gaps_ref, own_count):
    before = place_ref[0] * own_count
    lag = jnp.int32(0)
    for i in range(gaps_ref.shape[0] - own_count + 1):
        lag = lag + jnp.where(i < before, gaps_ref[i], 0)
    found = [lag]
    for i in range(own_count - 1):
        lag = lag + gaps_ref[before + i]
        found.append(lag)
    return found


def cut(value, out_ref):
    up = value.shape[0] // TALL
    for q in range(out_ref.shape[0]):
        j, a = q // up, q % up
        if j < value.shape[1] // WIDE:
            block = value[a * TALL:(a + 1) * TALL, j * WIDE:(j + 1) * WIDE]
        else:
            block = jnp.zeros((TALL, WIDE), value.dtype)
        out_ref[q] = block.astype(out_ref.dtype)


def forward_kernel(place_ref, gaps_ref, source_ref, green_ref, out_ref, early, total, lag_ref):
    step, last = pl.program_id(0), pl.num_programs(0) - 1
    rows, steps, cells = source_ref.shape
    nb = green_ref.shape[0]
    height = rows * steps
    lanes = early.shape[2]

    @pl.when(step == 0)
    def _():
        for k, lag in enumerate(lags(place_ref, gaps_ref, lag_ref.shape[0])):
            lag_ref[k] = lag
        for i in range(cells // lanes):
            early[i, pl.ds(0, height), :] = jnp.zeros((height, lanes), early.dtype)
            for r in range(rows):
                piece = source_ref[r, :, i * lanes:(i + 1) * lanes].astype(jnp.float32)
                early[i, pl.ds(height + r, steps, stride=rows), :] = piece

    shifted = []
    for k in range(nb):
        start = pl.multiple_of((steps - lag_ref[step * nb + k]) * rows, rows)
        for i in range(cells // lanes):
            shifted.append(early[i, pl.ds(start, height), :].astype(jnp.bfloat16))
    shifted = jnp.concatenate(shifted, axis=1)
    stored = jnp.concatenate([green_ref[k] for k in range(nb)], axis=1)
    part = lax.dot_general(shifted, stored, (((1,), (1,)), ((), ())), preferred_element_type=jnp.float32)

    if lag_ref.shape[0] // nb > 1:
        @pl.when(step == 0)
        def _():
            total[...] = part

        @pl.when(jnp.logical_and(step > 0, step < last))
        def _():
            total[...] += part

        @pl.when(step == last)
        def _():
            cut(total[...] + part, out_ref)
    else:
        cut(part, out_ref)


def forward(place, gaps, source, green, owners, nb, wire):
    rows, steps, cells = source.shape
    blocks, sensors, _ = green.shape
    height = rows * steps
    return pl.pallas_call(
        forward_kernel,
        grid_spec=pltpu.PrefetchScalarGridSpec(
            num_scalar_prefetch=2,
            grid=(blocks // nb,),
            in_specs=[
                pl.BlockSpec((rows, steps, cells), lambda k, *_: (0, 0, 0)),
                pl.BlockSpec((nb, sensors, cells), lambda k, *_: (k, 0, 0)),
            ],
            out_specs=pl.BlockSpec((owners, TALL, WIDE), lambda k, *_: (0, 0, 0)),
            scratch_shapes=[
                pltpu.VMEM((pl.cdiv(cells, 128), 2 * height, min(cells, 128)), jnp.float32),
                pltpu.VMEM((height, sensors), jnp.float32),
                pltpu.SMEM((blocks,), jnp.int32),
            ],
        ),
        out_shape=jax.ShapeDtypeStruct((owners, TALL, WIDE), wire),
        name="forward",
    )(place, gaps, source, green)


def adjoint_kernel(place_ref, gaps_ref, weighted_ref, green_ref, out_ref, flat, late, *, rows, nb):
    height, cells = out_ref.shape
    blocks, sensors, _ = green_ref.shape
    up = height // TALL
    lag = lags(place_ref, gaps_ref, blocks)
    flat[pl.ds(height, TALL), :] = jnp.zeros((TALL, sensors), flat.dtype)
    for q in range(up * (sensors // WIDE)):
        j, a = q // up, q % up
        block = weighted_ref[q]
        late[0, pl.ds(a * TALL, TALL), pl.ds(j * WIDE, WIDE)] = block
        flat[pl.ds(a * TALL, TALL), pl.ds(j * WIDE, WIDE)] = block.astype(jnp.float32)
    late[0, pl.ds(height, height), :] = jnp.zeros((height, sensors), late.dtype)
    late[1, pl.ds(0, height), :] = flat[pl.ds(rows, height), :].astype(late.dtype)
    late[1, pl.ds(height, height), :] = jnp.zeros((height, sensors), late.dtype)
    for part in range(blocks // nb):
        windows = []
        for k in range(part * nb, part * nb + nb):
            half = lax.shift_right_logical(lag[k], 1)
            start = pl.multiple_of(half * (2 * rows), 2 * rows)
            windows.append(late[lag[k] - 2 * half, pl.ds(start, height), :])
        held = green_ref[pl.ds(part * nb, nb)].reshape(nb * sensors, cells)
        value = jnp.dot(jnp.concatenate(windows, axis=1), held, preferred_element_type=jnp.float32)
        if part == 0:
            out_ref[...] = value.astype(out_ref.dtype)
        else:
            out_ref[...] = (out_ref[...] + value).astype(out_ref.dtype)


def adjoint(place, gaps, weighted, green, rows, steps, nb):
    blocks, sensors, cells = green.shape
    height = rows * steps
    return pl.pallas_call(
        functools.partial(adjoint_kernel, rows=rows, nb=nb),
        in_specs=[SMEM, SMEM, VMEM, VMEM],
        out_specs=VMEM,
        scratch_shapes=[
            pltpu.VMEM((height + TALL, sensors), jnp.float32),
            pltpu.VMEM((2, 2 * height, sensors), jnp.bfloat16),
        ],
        out_shape=jax.ShapeDtypeStruct((height, cells), jnp.float32),
        compiler_params=LIMIT,
        name="adjoint",
    )(place, gaps, weighted, green)


def body(green, source, observed, lag_gaps, huber_level):
    rows, steps, cells = source.shape
    sensors = green.shape[1]
    depth, owners, groups = lax.axis_size("z"), lax.axis_size(PLANE), lax.axis_size("y")
    slim = TALL // depth
    up = rows * steps // TALL
    place = lax.axis_index("y")[None]

    sent = forward(place, lag_gaps, source, green, owners, 4, WIRE)
    sent = lax.all_to_all(sent, PLANE, 0, 0, tiled=True)
    plane_sum = jnp.sum(sent.astype(jnp.float32), axis=0).reshape(depth, slim, WIDE)
    summed = jnp.sum(lax.all_to_all(plane_sum, "z", 0, 0, tiled=True), axis=0)

    block = jnp.minimum(lax.axis_index(PLANE), up * (sensors // WIDE) - 1)
    column = WIDE * lax.div(block, up)
    row = TALL * lax.rem(block, up) + slim * lax.axis_index("z")
    seen = lax.dynamic_slice(observed, (lax.rem(row, rows), lax.div(row, rows), column), (slim, 1, WIDE))
    seen = seen.reshape(slim, WIDE)
    level = lax.dynamic_slice(huber_level, (column,), (WIDE,))
    threshold = 0.3 * (level.astype(jnp.float32) + 1.0)[None]
    misfit = summed - seen
    own = (misfit * threshold / jnp.maximum(jnp.abs(misfit), threshold)).astype(jnp.bfloat16)

    own = lax.all_to_all(jnp.broadcast_to(own[None], (depth, slim, WIDE)), "z", 0, 0, tiled=True)
    own = jnp.broadcast_to(own.reshape(1, TALL, WIDE), (owners, TALL, WIDE))
    weighted = lax.all_to_all(own, PLANE, 0, 0, tiled=True)

    terms = adjoint(place, lag_gaps, weighted, green, rows, steps, 4)
    terms = terms.reshape(groups, steps // groups, rows, cells)
    terms = jnp.sum(lax.all_to_all(terms, "y", 0, 0, tiled=True), axis=0)
    return terms.transpose(1, 0, 2)


def solution(mesh):
    fine = Mesh(mesh.devices.reshape(16, 4, 2, 4), ("z", "x", "c", "y"))
    cell = ("z", "x", "c")
    in_specs = (P("y", None, cell), P(None, None, cell), P(), P(), P())
    out_specs = P(None, "y", cell)
    return jax.shard_map(body, mesh=fine, in_specs=in_specs, out_specs=out_specs, check_vma=False)
```

time: 553 us -> 96.2 us (0.17)
  waiting for transfers between devices: 485 us -> 9.86 us
  blocking collectives: 0 us -> 62.9 us
  between operations: 38.8 us -> 0.08 us
  matrix products: 21.9 us -> 0 us
  starting transfers between devices: 0.04 us -> 13 us
  Pallas kernels: 0 us -> 6.84 us
    psum x1 -> x0, waiting for transfers between devices: 462 us -> none  [body(): summed = lax.psum(predicted, ('cell', 'lag'))]
    all_to_all x0 -> x4, blocking collectives: none -> 62.9 us  [the longest x1 21.6 us: body(): sent = lax.all_to_all(sent, PLANE, 0, 0, tiled=True)]
    reduce_scatter x1 -> x0, waiting for transfers between devices: 22.9 us -> none  [body(): return lax.psum_scatter(terms, 'lag', scatter_dimension=1, tiled=True)]
    dot_general x16 -> x0, matrix products: 21.9 us -> none  [the longest x8 19.1 us: body(): jnp.einsum('rtc,sc->rts', shifted, green[block], preferred_element_type=j...]
    all_to_all x0 -> x1, starting transfers between devices: none -> 13 us  [body(): summed = jnp.sum(lax.all_to_all(plane_sum, 'z', 0, 0, tiled=True), axis=0)]
    all_to_all x0 -> x1, waiting for transfers between devices: none -> 9.86 us  [body(): summed = jnp.sum(lax.all_to_all(plane_sum, 'z', 0, 0, tiled=True), axis=0)]
    pallas_call x0 -> x2, Pallas kernels: none -> 6.84 us  [the longest x1 4.93 us: forward(): pl.pallas_call(forward_kernel, grid_spec=pltpu.PrefetchScalarGridSpec(num...]
  transfers between devices with their start and end apart: 2 -> 1, of which waited for: 2 -> 1; matrix products, arithmetic and copies ran while one was open for 0% -> 2% of each run, Pallas kernels for 0% -> 0%
where the time goes in v2:
time: 96.2 us; the launch traced here: 95.8 us
  blocking collectives  62.9 us (65%)
  starting transfers between devices  13 us (14%)
  waiting for transfers between devices  9.86 us (10%)
  Pallas kernels  6.84 us (7%)
  other arithmetic  2.16 us (2%)
    all_to_all x1, blocking collectives, body(): sent = lax.all_to_all(sent, PLANE, 0, 0, tiled=True)  21.6 us
    all_to_all x1, blocking collectives, body(): weighted = lax.all_to_all(own, PLANE, 0, 0, tiled=True)  17.9 us
    all_to_all x1, blocking collectives, body(): lax.all_to_all(jnp.broadcast_to(own[None], (depth, slim, WIDE)), 'z', 0,...  13.8 us
    all_to_all x1, starting transfers between devices, body(): summed = jnp.sum(lax.all_to_all(plane_sum, 'z', 0, 0, tiled=True), axis=0)  13 us
    all_to_all x1, waiting for transfers between devices, body(): summed = jnp.sum(lax.all_to_all(plane_sum, 'z', 0, 0, tiled=True), axis=0)  9.86 us
    all_to_all x1, blocking collectives, body(): terms = jnp.sum(lax.all_to_all(terms, 'y', 0, 0, tiled=True), axis=0)  9.58 us
    pallas_call x1, Pallas kernels, forward(): pl.pallas_call(forward_kernel, grid_spec=pltpu.PrefetchScalarGridSpec(num...  4.93 us
  transfers between devices with their start and end apart: 1, of which 1 were waited for; matrix products, arithmetic and copies ran while one was open for 2% of the time, Pallas kernels for 0%

profile of v2, /device:TPU:1, one launch (start us, length us, event | category | flops | bytes accessed | tf_op | source)
XLA Modules:
  0.0 95.8 jit_solution(2391196618745846651)
XLA Ops:
  0.0 0.0 copy-start
  0.0 0.0 copy-start.1
  0.0 4.9 %forward.1 = bf16[32,64,128]{2,1,0:T(8,128)(2,1)} custom-call(s32[1]{0:T(128)} %bitcast.place_ref, s32[31]{0:T(128)} %gaps_ref.3, bf16[8,48,256]{2,1,0:T(8,128)(2,1)} %source_ref.1, bf16[8,640,256]{2,1,0:T(8,128)(2,1)} %green_ref.3), custom_call_target="tpu_custom_call" | custom-call | tf_op jit(solution)/shard_map/forward/pallas_call | solution.py:87
  4.9 21.6 %all_to_all.25 = bf16[32,64,128]{2,1,0:T(8,128)(2,1)S(1)} all-to-all(bf16[32,64,128]{2,1,0:T(8,128)(2,1)} %forward.1), channel_id=1, replica_groups=mesh['z'=16,'x'=4,'c'=2,'y'=4] {'x','c','y'}, dimensions={0} | all-to-all | bytes 1048576 | tf_op jit(solution)/shard_map/all_to_all | solution.py:162
  26.5 0.7 convert_reduce_fusion
  27.2 13.0 %all-to-all-start.1 = ((f32[16,4,128]{2,1,0:T(4,128)}), f32[16,4,128]{2,1,0:T(4,128)S(1)}, u32[]{:S(2)}, u32[]{:S(2)}) async-start(f32[16,4,128]{2,1,0:T(4,128)} %bitcast.1), calls=%async_computation.1 | async-start | bytes 65536 | tf_op jit(solution)/shard_map/all_to_all | solution.py:164
  40.3 0.8 dynamic_slice.6
  41.1 0.8 add_multiply_fusion
  41.8 9.9 %all-to-all-done.1 = f32[16,4,128]{2,1,0:T(4,128)S(1)} async-done(((f32[16,4,128]{2,1,0:T(4,128)}), f32[16,4,128]{2,1,0:T(4,128)S(1)}, u32[]{:S(2)}, u32[]{:S(2)}) %all-to-all-start.1) | async-done | bytes 32800 | tf_op jit(solution)/shard_map/all_to_all | solution.py:164
  51.8 13.8 %all_to_all.26 = bf16[16,4,128]{2,1,0:T(4,128)(2,1)S(1)} all-to-all(bf16[16,4,128]{2,1,0:T(4,128)(2,1)S(1)} %broadcast_in_dim.18), channel_id=1, replica_groups=mesh['z'=16,'x'=4,'c'=2,'y'=4] {'z'}, dimensions={0} | all-to-all | bytes 32768 | tf_op jit(solution)/shard_map/all_to_all | solution.py:176
  65.6 0.1 broadcast_in_dim.20
  65.7 17.9 %all_to_all.27.weighted_ref = bf16[32,64,128]{2,1,0:T(8,128)(2,1)S(1)} all-to-all(bf16[32,64,128]{2,1,0:T(8,128)(2,1)S(1)} %broadcast_in_dim.20), channel_id=1, replica_groups=mesh['z'=16,'x'=4,'c'=2,'y'=4] {'x','c','y'}, dimensions={0} | all-to-all | bytes 1048576 | tf_op jit(solution)/shard_map/all_to_all | solution.py:178
  83.6 0.0 copy-done
  83.6 0.0 copy-done.1
  83.6 1.9 %adjoint.1 = f32[384,256]{1,0:T(8,128)S(1)} custom-call(s32[1]{0:T(128)} %bitcast.place_ref, s32[31]{0:T(128)S(1)} %copy-done.1, bf16[32,64,128]{2,1,0:T(8,128)(2,1)S(1)} %all_to_all.27.weighted_ref, bf16[8,640,256]{2,1,0:T(8,128)(2,1)S(1)} %copy-done), custom_call_target="tpu_custom_call" | custom-call | tf_op jit(solution)/shard_map/adjoint/pallas_call | solution.py:139
  85.5 9.6 %all_to_all.28 = f32[4,12,8,256]{3,2,1,0:T(8,128)S(1)} all-to-all(f32[4,12,8,256]{3,2,1,0:T(8,128)S(1)} %bitcast.6), channel_id=1, replica_groups=mesh['z'=16,'x'=4,'c'=2,'y'=4] {'y'}, dimensions={0} | all-to-all | bytes 786432 | tf_op jit(solution)/shard_map/all_to_all | solution.py:182
  95.1 0.7 reduce_sum.29
  (3 shorter events, 0.0 us)
Async XLA Ops:
  0.0 83.6 %copy-start = (bf16[8,640,256]{2,1,0:T(8,128)(2,1)S(1)}, bf16[8,640,256]{2,1,0:T(8,128)(2,1)}, u32[]{:S(2)}) copy-start(bf16[8,640,256]{2,1,0:T(8,128)(2,1)} %green_ref.3) | copy-start | bytes 7864324
  0.0 83.6 %copy-start.1 = (s32[31]{0:T(128)S(1)}, s32[31]{0:T(128)}, u32[]{:S(2)}) copy-start(s32[31]{0:T(128)} %gaps_ref.3) | copy-start | bytes 376
  27.2 24.5 %all-to-all-start.1 = ((f32[16,4,128]{2,1,0:T(4,128)}), f32[16,4,128]{2,1,0:T(4,128)S(1)}, u32[]{:S(2)}, u32[]{:S(2)}) async-start(f32[16,4,128]{2,1,0:T(4,128)} %bitcast.1), calls=%async_computation.1 | async-start | bytes 65536 | tf_op jit(solution)/shard_map/all_to_all | solution.py:164

commit v3 on v2

v3 whole, which is shorter than its diff:
```python
import functools
import jax
import jax.numpy as jnp
from jax import lax
from jax.experimental import pallas as pl
from jax.experimental.pallas import tpu as pltpu
from jax.sharding import Mesh, PartitionSpec as P

PLANE = ("x", "c", "y")
TALL, WIDE = 64, 128
WIRE = jnp.bfloat16
VMEM = pl.BlockSpec(memory_space=pltpu.VMEM)
SMEM = pl.BlockSpec(memory_space=pltpu.SMEM)
HBM = pl.BlockSpec(memory_space=pl.ANY)
LIMIT = pltpu.CompilerParams(vmem_limit_bytes=20 << 20)


def lags(place_ref, gaps_ref, own_count):
    before = place_ref[0] * own_count
    lag = jnp.int32(0)
    for i in range(gaps_ref.shape[0] - own_count + 1):
        lag = lag + jnp.where(i < before, gaps_ref[i], 0)
    found = [lag]
    for i in range(own_count - 1):
        lag = lag + gaps_ref[before + i]
        found.append(lag)
    return found


def forward_kernel(
    place_ref, owner_ref, gaps_ref, source_ref, green_ref, observed_ref, out_ref, seen_ref, gaps, source, green, early, total, sems, *, nb
):
    rows, steps, cells = source.shape
    blocks, sensors, _ = green.shape
    height = rows * steps
    up = height // TALL
    lanes = early.shape[2]
    parts = blocks // nb
    gaps_in = pltpu.make_async_copy(gaps_ref, gaps, sems.at[0])
    source_in = pltpu.make_async_copy(source_ref, source, sems.at[1])
    gaps_in.start()
    source_in.start()
    green_in = []
    for part in range(parts):
        at = pl.ds(part * nb, nb)
        green_in.append(pltpu.make_async_copy(green_ref.at[at], green.at[at], sems.at[2 + part]))
        green_in[-1].start()
    own = jnp.minimum(owner_ref[0], up * (sensors // WIDE) - 1)
    when = pl.ds(pl.multiple_of(lax.rem(own, up) * (TALL // rows), TALL // rows), TALL // rows)
    column = pl.ds(pl.multiple_of(lax.div(own, up) * WIDE, WIDE), WIDE)
    seen_in = pltpu.make_async_copy(observed_ref.at[:, when, column], seen_ref, sems.at[2 + parts])
    seen_in.start()
    early[:, pl.ds(0, height), :] = jnp.zeros((early.shape[0], height, lanes), early.dtype)
    gaps_in.wait()
    lag = lags(place_ref, gaps, blocks)
    source_in.wait()
    for i in range(cells // lanes):
        for r in range(rows):
            piece = source[r, :, i * lanes:(i + 1) * lanes].astype(jnp.float32)
            early[i, pl.ds(height + r, steps, stride=rows), :] = piece

    for part in range(parts):
        shifted, held = [], []
        green_in[part].wait()
        for k in range(part * nb, part * nb + nb):
            start = pl.multiple_of((steps - lag[k]) * rows, rows)
            for i in range(cells // lanes):
                shifted.append(early[i, pl.ds(start, height), :].astype(jnp.bfloat16))
            held.append(green[k])
        value = lax.dot_general(
            jnp.concatenate(shifted, axis=1), jnp.concatenate(held, axis=1),
            (((1,), (1,)), ((), ())), preferred_element_type=jnp.float32,
        )
        if part > 0:
            value = total[...] + value
        if part < parts - 1:
            total[...] = value
    for q in range(out_ref.shape[0]):
        j, a = q // up, q % up
        if j < value.shape[1] // WIDE:
            block = value[a * TALL:(a + 1) * TALL, j * WIDE:(j + 1) * WIDE]
        else:
            block = jnp.zeros((TALL, WIDE), value.dtype)
        out_ref[q] = block.astype(out_ref.dtype)
    seen_in.wait()


def forward(place, owner, gaps, source, green, observed, owners, nb, wire):
    rows, steps, cells = source.shape
    blocks, sensors, _ = green.shape
    height = rows * steps
    return pl.pallas_call(
        functools.partial(forward_kernel, nb=nb),
        in_specs=[SMEM, SMEM, HBM, HBM, HBM, HBM],
        out_specs=[VMEM, VMEM],
        scratch_shapes=[
            pltpu.SMEM(gaps.shape, gaps.dtype),
            pltpu.VMEM(source.shape, source.dtype),
            pltpu.VMEM(green.shape, green.dtype),
            pltpu.VMEM((pl.cdiv(cells, 128), 2 * height, min(cells, 128)), jnp.float32),
            pltpu.VMEM((height, sensors), jnp.float32),
            pltpu.SemaphoreType.DMA((3 + blocks // nb,)),
        ],
        out_shape=[
            jax.ShapeDtypeStruct((owners, TALL, WIDE), wire),
            jax.ShapeDtypeStruct((rows, TALL // rows, WIDE), observed.dtype),
        ],
        name="forward",
    )(place, owner, gaps, source, green, observed)


def plane_kernel(parts_ref, out_ref):
    value = parts_ref[0].astype(jnp.float32)
    for q in range(1, parts_ref.shape[0]):
        value = value + parts_ref[q].astype(jnp.float32)
    value = value.astype(out_ref.dtype)
    for p in range(out_ref.shape[0]):
        out_ref[p] = value


def plane_sum(parts, copies, wire):
    return pl.pallas_call(
        plane_kernel,
        in_specs=[VMEM],
        out_specs=VMEM,
        out_shape=jax.ShapeDtypeStruct((copies,) + parts.shape[1:], wire),
        compiler_params=LIMIT,
        name="plane_sum",
    )(parts)


def weigh_kernel(parts_ref, seen_ref, level_ref, out_ref):
    value = parts_ref[0].astype(jnp.float32)
    for p in range(1, parts_ref.shape[0]):
        value = value + parts_ref[p].astype(jnp.float32)
    threshold = 0.3 * (level_ref[...].astype(jnp.float32) + 1.0)
    misfit = value - seen_ref[...]
    weighted = (misfit * threshold / jnp.maximum(jnp.abs(misfit), threshold)).astype(out_ref.dtype)
    for q in range(out_ref.shape[0]):
        out_ref[q] = weighted


def weigh(parts, seen, level, copies):
    return pl.pallas_call(
        weigh_kernel,
        in_specs=[VMEM, VMEM, VMEM],
        out_specs=VMEM,
        out_shape=jax.ShapeDtypeStruct((copies,) + parts.shape[1:], jnp.bfloat16),
        compiler_params=LIMIT,
        name="weigh",
    )(parts, seen, level)


def adjoint_kernel(place_ref, gaps_ref, weighted_ref, green_ref, out_ref, flat, late, *, rows, nb):
    height, cells = out_ref.shape
    blocks, sensors, _ = green_ref.shape
    up = height // TALL
    lag = lags(place_ref, gaps_ref, blocks)
    flat[pl.ds(height, TALL), :] = jnp.zeros((TALL, sensors), flat.dtype)
    for q in range(up * (sensors // WIDE)):
        j, a = q // up, q % up
        block = weighted_ref[q]
        late[0, pl.ds(a * TALL, TALL), pl.ds(j * WIDE, WIDE)] = block
        flat[pl.ds(a * TALL, TALL), pl.ds(j * WIDE, WIDE)] = block.astype(jnp.float32)
    late[0, pl.ds(height, height), :] = jnp.zeros((height, sensors), late.dtype)
    late[1, pl.ds(0, height), :] = flat[pl.ds(rows, height), :].astype(late.dtype)
    late[1, pl.ds(height, height), :] = jnp.zeros((height, sensors), late.dtype)
    for part in range(blocks // nb):
        windows = []
        for k in range(part * nb, part * nb + nb):
            half = lax.shift_right_logical(lag[k], 1)
            start = pl.multiple_of(half * (2 * rows), 2 * rows)
            windows.append(late[lag[k] - 2 * half, pl.ds(start, height), :])
        held = green_ref[pl.ds(part * nb, nb)].reshape(nb * sensors, cells)
        value = jnp.dot(jnp.concatenate(windows, axis=1), held, preferred_element_type=jnp.float32)
        if part == 0:
            out_ref[...] = value.astype(out_ref.dtype)
        else:
            out_ref[...] = (out_ref[...] + value).astype(out_ref.dtype)


def adjoint(place, gaps, weighted, green, rows, steps, nb):
    blocks, sensors, cells = green.shape
    height = rows * steps
    return pl.pallas_call(
        functools.partial(adjoint_kernel, rows=rows, nb=nb),
        in_specs=[SMEM, SMEM, VMEM, VMEM],
        out_specs=VMEM,
        scratch_shapes=[
            pltpu.VMEM((height + TALL, sensors), jnp.float32),
            pltpu.VMEM((2, 2 * height, sensors), jnp.bfloat16),
        ],
        out_shape=jax.ShapeDtypeStruct((height, cells), jnp.float32),
        compiler_params=LIMIT,
        name="adjoint",
    )(place, gaps, weighted, green)


def body(green, source, observed, lag_gaps, huber_level):
    rows, steps, cells = source.shape
    sensors = green.shape[1]
    depth, owners, groups = lax.axis_size("z"), lax.axis_size(PLANE), lax.axis_size("y")
    place, owner = lax.axis_index("y")[None], lax.axis_index(PLANE)[None]

    parts, seen = forward(place, owner, lag_gaps, source, green, observed, owners, 8, WIRE)
    parts = lax.all_to_all(parts, PLANE, 0, 0, tiled=True)
    planes = lax.all_to_all(plane_sum(parts, depth, WIRE), "z", 0, 0, tiled=True)

    column = WIDE * lax.div(lax.axis_index(PLANE), rows * steps // TALL)
    level = lax.dynamic_slice(huber_level, (jnp.minimum(column, sensors - WIDE),), (WIDE,))[None]
    seen = seen.transpose(1, 0, 2).reshape(TALL, WIDE)
    weighted = weigh(planes, seen, level, owners)
    weighted = lax.all_to_all(weighted, PLANE, 0, 0, tiled=True)

    terms = adjoint(place, lag_gaps, weighted, green, rows, steps, 4)
    terms = terms.reshape(groups, steps // groups, rows, cells)
    terms = jnp.sum(lax.all_to_all(terms, "y", 0, 0, tiled=True), axis=0)
    return terms.transpose(1, 0, 2)


def solution(mesh):
    fine = Mesh(mesh.devices.reshape(16, 4, 2, 4), ("z", "x", "c", "y"))
    cell = ("z", "x", "c")
    in_specs = (P("y", None, cell), P(None, None, cell), P(), P(), P())
    out_specs = P(None, "y", cell)
    return jax.shard_map(body, mesh=fine, in_specs=in_specs, out_specs=out_specs, check_vma=False)
```

time: 96.2 us -> 86.1 us (0.90)
  blocking collectives: 62.9 us -> 52.1 us
  waiting for transfers between devices: 9.86 us -> 12.1 us
  other arithmetic: 2.16 us -> 0.66 us
    all_to_all x3 -> x2, blocking collectives: 53.3 us -> 42.5 us  [the longest x1 21.7 us: body(): parts = lax.all_to_all(parts, PLANE, 0, 0, tiled=True)]
    all_to_all x1, waiting for transfers between devices: 9.86 us -> 12.1 us  [body(): lax.all_to_all(plane_sum(parts, depth, WIRE), 'z', 0, 0, tiled=True)]
    pallas_call x1 -> x3, Pallas kernels: 4.93 us -> 5.01 us  [the longest x1 4.14 us: forward(): pl.pallas_call(functools.partial(forward_kernel, nb=nb), in_specs=[SMEM,...]
  transfers between devices with their start and end apart: 1 -> 1, of which waited for: 1 -> 1; matrix products, arithmetic and copies ran while one was open for 2% -> 1% of each run, Pallas kernels for 0% -> 0%
where the time goes in v3:
time: 86.1 us; the launch traced here: 85.7 us
  blocking collectives  52.1 us (61%)
  starting transfers between devices  13 us (15%)
  waiting for transfers between devices  12.1 us (14%)
  Pallas kernels  6.92 us (8%)
    all_to_all x1, blocking collectives, body(): parts = lax.all_to_all(parts, PLANE, 0, 0, tiled=True)  21.7 us
    all_to_all x1, blocking collectives, body(): weighted = lax.all_to_all(weighted, PLANE, 0, 0, tiled=True)  20.8 us
    all_to_all x1, starting transfers between devices, body(): lax.all_to_all(plane_sum(parts, depth, WIRE), 'z', 0, 0, tiled=True)  13 us
    all_to_all x1, waiting for transfers between devices, body(): lax.all_to_all(plane_sum(parts, depth, WIRE), 'z', 0, 0, tiled=True)  12.1 us
    all_to_all x1, blocking collectives, body(): terms = jnp.sum(lax.all_to_all(terms, 'y', 0, 0, tiled=True), axis=0)  9.58 us
    pallas_call x1, Pallas kernels, forward(): pl.pallas_call(functools.partial(forward_kernel, nb=nb), in_specs=[SMEM,...  4.14 us
    pallas_call x1, Pallas kernels, adjoint(): pl.pallas_call(functools.partial(adjoint_kernel, rows=rows, nb=nb), in_sp...  1.91 us
  transfers between devices with their start and end apart: 1, of which 1 were waited for; matrix products, arithmetic and copies ran while one was open for 1% of the time, Pallas kernels for 0%

profile of v3, /device:TPU:1, one launch (start us, length us, event | category | flops | bytes accessed | tf_op | source)
XLA Modules:
  0.0 85.7 jit_solution(15602210703738153087)
XLA Ops:
  0.0 0.0 copy-start
  0.0 4.1 %forward.1 = (bf16[32,64,128]{2,1,0:T(8,128)(2,1)}, f32[8,8,128]{2,1,0:T(8,128)}) custom-call(s32[1]{0:T(128)} %bitcast.place_ref, s32[1]{0:T(128)} %bitcast.1.owner_ref, s32[31]{0:T(128)} %gaps_ref.3, bf16[8,48,256]{2,1,0:T(8,128)(2,1)} %source_ref.1, bf16[8,640,256]{2,1,0:T(8,128)(2,1)} %green_ref.3, f32[8,48,640]{2,1,0:T(8,128)} %observed_ref.1), custom_call_target="tpu_custom_call" | custom-call | tf_op jit(solution)/shard_map/forward/pallas_call | solution.py:92
  4.2 0.0 copy-start.1
  4.2 0.0 copy-start.2
  4.2 21.7 %all_to_all.20.parts_ref = bf16[32,64,128]{2,1,0:T(8,128)(2,1)S(1)} all-to-all(bf16[32,64,128]{2,1,0:T(8,128)(2,1)} %get-tuple-element.7), channel_id=1, replica_groups=mesh['z'=16,'x'=4,'c'=2,'y'=4] {'x','c','y'}, dimensions={0} | all-to-all | bytes 1048576 | tf_op jit(solution)/shard_map/all_to_all | solution.py:206
  25.9 0.8 plane_sum.1
  26.7 13.0 %all-to-all-start.1 = ((bf16[16,64,128]{2,1,0:T(8,128)(2,1)}), bf16[16,64,128]{2,1,0:T(8,128)(2,1)S(1)}, u32[]{:S(2)}, u32[]{:S(2)}) async-start(bf16[16,64,128]{2,1,0:T(8,128)(2,1)} %plane_sum.1), calls=%async_computation.1 | async-start | bytes 524288 | tf_op jit(solution)/shard_map/all_to_all | solution.py:207
  39.7 0.8 copy.8
  40.5 0.0 copy-done
  40.5 0.1 dynamic-slice_bitcast_fusion.level_ref
  40.6 12.1 %all-to-all-done.1.parts_ref = bf16[16,64,128]{2,1,0:T(8,128)(2,1)S(1)} async-done(((bf16[16,64,128]{2,1,0:T(8,128)(2,1)}), bf16[16,64,128]{2,1,0:T(8,128)(2,1)S(1)}, u32[]{:S(2)}, u32[]{:S(2)}) %all-to-all-start.1) | async-done | bytes 262176 | tf_op jit(solution)/shard_map/all_to_all | solution.py:207
  52.7 0.1 weigh.1
  52.7 20.8 %all_to_all.21.weighted_ref = bf16[32,64,128]{2,1,0:T(8,128)(2,1)S(1)} all-to-all(bf16[32,64,128]{2,1,0:T(8,128)(2,1)S(1)} %weigh.1), channel_id=1, replica_groups=mesh['z'=16,'x'=4,'c'=2,'y'=4] {'x','c','y'}, dimensions={0} | all-to-all | bytes 1048576 | tf_op jit(solution)/shard_map/all_to_all | solution.py:213
  73.5 0.0 copy-done.1
  73.5 0.0 copy-done.2
  73.5 1.9 %adjoint.1 = f32[384,256]{1,0:T(8,128)S(1)} custom-call(s32[1]{0:T(128)} %bitcast.place_ref, s32[31]{0:T(128)S(1)} %copy-done.2, bf16[32,64,128]{2,1,0:T(8,128)(2,1)S(1)} %all_to_all.21.weighted_ref, bf16[8,640,256]{2,1,0:T(8,128)(2,1)S(1)} %copy-done.1), custom_call_target="tpu_custom_call" | custom-call | tf_op jit(solution)/shard_map/adjoint/pallas_call | solution.py:185
  75.4 9.6 %all_to_all.22 = f32[4,12,8,256]{3,2,1,0:T(8,128)S(1)} all-to-all(f32[4,12,8,256]{3,2,1,0:T(8,128)S(1)} %bitcast.10), channel_id=1, replica_groups=mesh['z'=16,'x'=4,'c'=2,'y'=4] {'y'}, dimensions={0} | all-to-all | bytes 786432 | tf_op jit(solution)/shard_map/all_to_all | solution.py:217
  85.0 0.7 reduce_sum.9
Async XLA Ops:
  0.0 40.5 %copy-start = (s32[640]{0:T(1024)S(1)}, s32[640]{0:T(1024)}, u32[]{:S(2)}) copy-start(s32[640]{0:T(1024)} %param.9) | copy-start | bytes 7684
  4.2 69.4 %copy-start.1 = (bf16[8,640,256]{2,1,0:T(8,128)(2,1)S(1)}, bf16[8,640,256]{2,1,0:T(8,128)(2,1)}, u32[]{:S(2)}) copy-start(bf16[8,640,256]{2,1,0:T(8,128)(2,1)} %green_ref.3) | copy-start | bytes 7864324
  4.2 69.4 %copy-start.2 = (s32[31]{0:T(128)S(1)}, s32[31]{0:T(128)}, u32[]{:S(2)}) copy-start(s32[31]{0:T(128)} %gaps_ref.3) | copy-start | bytes 376
  26.7 26.0 %all-to-all-start.1 = ((bf16[16,64,128]{2,1,0:T(8,128)(2,1)}), bf16[16,64,128]{2,1,0:T(8,128)(2,1)S(1)}, u32[]{:S(2)}, u32[]{:S(2)}) async-start(bf16[16,64,128]{2,1,0:T(8,128)(2,1)} %plane_sum.1), calls=%async_computation.1 | async-start | bytes 524288 | tf_op jit(solution)/shard_map/all_to_all | solution.py:207

commit v4 on v3

--- a/solution.py
+++ b/solution.py
@@ -28,28 +28,28 @@
 
 
 def forward_kernel(
-    place_ref, owner_ref, gaps_ref, source_ref, green_ref, observed_ref, out_ref, seen_ref, gaps, source, green, early, total, sems, *, nb
+    place_ref, owner_ref, gaps_ref, source_ref, green_ref, observed_ref, level_ref,
+    out_ref, side_ref, gaps, source, green, early, seen, level, sems
 ):
     rows, steps, cells = source.shape
     blocks, sensors, _ = green.shape
     height = rows * steps
     up = height // TALL
     lanes = early.shape[2]
-    parts = blocks // nb
     gaps_in = pltpu.make_async_copy(gaps_ref, gaps, sems.at[0])
     source_in = pltpu.make_async_copy(source_ref, source, sems.at[1])
     gaps_in.start()
     source_in.start()
-    green_in = []
-    for part in range(parts):
-        at = pl.ds(part * nb, nb)
-        green_in.append(pltpu.make_async_copy(green_ref.at[at], green.at[at], sems.at[2 + part]))
-        green_in[-1].start()
+    green_in = pltpu.make_async_copy(green_ref, green, sems.at[2])
+    green_in.start()
     own = jnp.minimum(owner_ref[0], up * (sensors // WIDE) - 1)
+    column = lax.div(own, up)
     when = pl.ds(pl.multiple_of(lax.rem(own, up) * (TALL // rows), TALL // rows), TALL // rows)
-    column = pl.ds(pl.multiple_of(lax.div(own, up) * WIDE, WIDE), WIDE)
-    seen_in = pltpu.make_async_copy(observed_ref.at[:, when, column], seen_ref, sems.at[2 + parts])
+    where = pl.ds(pl.multiple_of(column * WIDE, WIDE), WIDE)
+    seen_in = pltpu.make_async_copy(observed_ref.at[:, when, where], seen, sems.at[3])
     seen_in.start()
+    level_in = pltpu.make_async_copy(level_ref, level, sems.at[4])
+    level_in.start()
     early[:, pl.ds(0, height), :] = jnp.zeros((early.shape[0], height, lanes), early.dtype)
     gaps_in.wait()
     lag = lags(place_ref, gaps, blocks)
@@ -59,22 +59,16 @@
             piece = source[r, :, i * lanes:(i + 1) * lanes].astype(jnp.float32)
             early[i, pl.ds(height + r, steps, stride=rows), :] = piece
 
-    for part in range(parts):
-        shifted, held = [], []
-        green_in[part].wait()
-        for k in range(part * nb, part * nb + nb):
-            start = pl.multiple_of((steps - lag[k]) * rows, rows)
-            for i in range(cells // lanes):
-                shifted.append(early[i, pl.ds(start, height), :].astype(jnp.bfloat16))
-            held.append(green[k])
-        value = lax.dot_general(
-            jnp.concatenate(shifted, axis=1), jnp.concatenate(held, axis=1),
-            (((1,), (1,)), ((), ())), preferred_element_type=jnp.float32,
-        )
-        if part > 0:
-            value = total[...] + value
-        if part < parts - 1:
-            total[...] = value
+    shifted = []
+    for k in range(blocks):
+        start = pl.multiple_of((steps - lag[k]) * rows, rows)
+        for i in range(cells // lanes):
+            shifted.append(early[i, pl.ds(start, height), :].astype(jnp.bfloat16))
+    green_in.wait()
+    value = lax.dot_general(
+        jnp.concatenate(shifted, axis=1), jnp.concatenate([green[k] for k in range(blocks)], axis=1),
+        (((1,), (1,)), ((), ())), preferred_element_type=jnp.float32,
+    )
     for q in range(out_ref.shape[0]):
         j, a = q // up, q % up
         if j < value.shape[1] // WIDE:
@@ -83,30 +77,37 @@
             block = jnp.zeros((TALL, WIDE), value.dtype)
         out_ref[q] = block.astype(out_ref.dtype)
     seen_in.wait()
-
-
-def forward(place, owner, gaps, source, green, observed, owners, nb, wire):
+    level_in.wait()
+    tall = TALL // rows
+    for r in range(rows):
+        side_ref[pl.ds(r, tall, stride=rows), :] = seen[r]
+    threshold = 0.3 * (level[pl.ds(column, 1), :].astype(jnp.float32) + 1.0)
+    side_ref[pl.ds(TALL, 8), :] = jnp.broadcast_to(threshold, (8, WIDE))
+
+
+def forward(place, owner, gaps, source, green, observed, level, owners, wire):
     rows, steps, cells = source.shape
     blocks, sensors, _ = green.shape
     height = rows * steps
     return pl.pallas_call(
-        functools.partial(forward_kernel, nb=nb),
-        in_specs=[SMEM, SMEM, HBM, HBM, HBM, HBM],
+        forward_kernel,
+        in_specs=[SMEM, SMEM, HBM, HBM, HBM, HBM, HBM],
         out_specs=[VMEM, VMEM],
         scratch_shapes=[
             pltpu.SMEM(gaps.shape, gaps.dtype),
             pltpu.VMEM(source.shape, source.dtype),
             pltpu.VMEM(green.shape, green.dtype),
             pltpu.VMEM((pl.cdiv(cells, 128), 2 * height, min(cells, 128)), jnp.float32),
-            pltpu.VMEM((height, sensors), jnp.float32),
-            pltpu.SemaphoreType.DMA((3 + blocks // nb,)),
+            pltpu.VMEM((rows, TALL // rows, WIDE), observed.dtype),
+            pltpu.VMEM(level.shape, level.dtype),
+            pltpu.SemaphoreType.DMA((5,)),
         ],
         out_shape=[
             jax.ShapeDtypeStruct((owners, TALL, WIDE), wire),
-            jax.ShapeDtypeStruct((rows, TALL // rows, WIDE), observed.dtype),
+            jax.ShapeDtypeStruct((TALL + 8, WIDE), observed.dtype),
         ],
         name="forward",
-    )(place, owner, gaps, source, green, observed)
+    )(place, owner, gaps, source, green, observed, level)
 
 
 def plane_kernel(parts_ref, out_ref):
@@ -129,26 +130,31 @@
     )(parts)
 
 
-def weigh_kernel(parts_ref, seen_ref, level_ref, out_ref):
+def weigh_kernel(parts_ref, side_ref, out_ref, side, sem):
+    side_in = pltpu.make_async_copy(side_ref, side, sem)
+    side_in.start()
     value = parts_ref[0].astype(jnp.float32)
     for p in range(1, parts_ref.shape[0]):
         value = value + parts_ref[p].astype(jnp.float32)
-    threshold = 0.3 * (level_ref[...].astype(jnp.float32) + 1.0)
-    misfit = value - seen_ref[...]
+    side_in.wait()
+    tall = parts_ref.shape[1]
+    misfit = value - side[pl.ds(0, tall), :]
+    threshold = side[pl.ds(tall, 1), :]
     weighted = (misfit * threshold / jnp.maximum(jnp.abs(misfit), threshold)).astype(out_ref.dtype)
     for q in range(out_ref.shape[0]):
         out_ref[q] = weighted
 
 
-def weigh(parts, seen, level, copies):
+def weigh(parts, side, copies):
     return pl.pallas_call(
         weigh_kernel,
-        in_specs=[VMEM, VMEM, VMEM],
+        in_specs=[VMEM, HBM],
         out_specs=VMEM,
+        scratch_shapes=[pltpu.VMEM(side.shape, side.dtype), pltpu.SemaphoreType.DMA],
         out_shape=jax.ShapeDtypeStruct((copies,) + parts.shape[1:], jnp.bfloat16),
         compiler_params=LIMIT,
         name="weigh",
-    )(parts, seen, level)
+    )(parts, side)
 
 
 def adjoint_kernel(place_ref, gaps_ref, weighted_ref, green_ref, out_ref, flat, late, *, rows, nb):
@@ -202,14 +208,12 @@
     depth, owners, groups = lax.axis_size("z"), lax.axis_size(PLANE), lax.axis_size("y")
     place, owner = lax.axis_index("y")[None], lax.axis_index(PLANE)[None]
 
-    parts, seen = forward(place, owner, lag_gaps, source, green, observed, owners, 8, WIRE)
+    level = huber_level.reshape(sensors // WIDE, WIDE)
+    parts, side = forward(place, owner, lag_gaps, source, green, observed, level, owners, WIRE)
     parts = lax.all_to_all(parts, PLANE, 0, 0, tiled=True)
     planes = lax.all_to_all(plane_sum(parts, depth, WIRE), "z", 0, 0, tiled=True)
 
-    column = WIDE * lax.div(lax.axis_index(PLANE), rows * steps // TALL)
-    level = lax.dynamic_slice(huber_level, (jnp.minimum(column, sensors - WIDE),), (WIDE,))[None]
-    seen = seen.transpose(1, 0, 2).reshape(TALL, WIDE)
-    weighted = weigh(planes, seen, level, owners)
+    weighted = weigh(planes, side, owners)
     weighted = lax.all_to_all(weighted, PLANE, 0, 0, tiled=True)
 
     terms = adjoint(place, lag_gaps, weighted, green, rows, steps, 4)

time: 86.1 us -> 86 us (level)
  blocking collectives: 52.1 us -> 77.8 us
  starting transfers between devices: 13 us -> 0 us
  waiting for transfers between devices: 12.1 us -> 0 us
    all_to_all x0 -> x1, blocking collectives: none -> 25.8 us  [body(): lax.all_to_all(plane_sum(parts, depth, WIRE), 'z', 0, 0, tiled=True)]
    all_to_all x1 -> x0, starting transfers between devices: 13 us -> none  [body(): lax.all_to_all(plane_sum(parts, depth, WIRE), 'z', 0, 0, tiled=True)]
    all_to_all x1 -> x0, waiting for transfers between devices: 12.1 us -> none  [body(): lax.all_to_all(plane_sum(parts, depth, WIRE), 'z', 0, 0, tiled=True)]
  transfers between devices with their start and end apart: 1 -> 0, of which waited for: 1 -> 0; matrix products, arithmetic and copies ran while one was open for 1% -> 0% of each run, Pallas kernels for 0% -> 0%
where the time goes in v4:
time: 86 us; the launch traced here: 85.6 us
  blocking collectives  77.8 us (90%)
  Pallas kernels  6.23 us (7%)
    all_to_all x1, blocking collectives, body(): lax.all_to_all(plane_sum(parts, depth, WIRE), 'z', 0, 0, tiled=True)  25.8 us
    all_to_all x1, blocking collectives, body(): parts = lax.all_to_all(parts, PLANE, 0, 0, tiled=True)  21.7 us
    all_to_all x1, blocking collectives, body(): weighted = lax.all_to_all(weighted, PLANE, 0, 0, tiled=True)  20.8 us
    all_to_all x1, blocking collectives, body(): terms = jnp.sum(lax.all_to_all(terms, 'y', 0, 0, tiled=True), axis=0)  9.58 us
    pallas_call x1, Pallas kernels, forward(): pl.pallas_call(forward_kernel, in_specs=[SMEM, SMEM, HBM, HBM, HBM, HBM,...  4.11 us
    pallas_call x1, Pallas kernels, adjoint(): pl.pallas_call(functools.partial(adjoint_kernel, rows=rows, nb=nb), in_sp...  1.9 us

profile of v4, /device:TPU:1, one launch (start us, length us, event | category | flops | bytes accessed | tf_op | source)
XLA Modules:
  0.0 85.6 jit_solution(6570098066854000538)
XLA Ops:
  0.0 0.0 copy-start.2
  0.0 4.1 %forward.1 = (bf16[32,64,128]{2,1,0:T(8,128)(2,1)}, f32[72,128]{1,0:T(8,128)}) custom-call(s32[1]{0:T(128)} %bitcast.place_ref, s32[1]{0:T(128)} %bitcast.1.owner_ref, s32[31]{0:T(128)} %gaps_ref.3, bf16[8,48,256]{2,1,0:T(8,128)(2,1)} %source_ref.1, bf16[8,640,256]{2,1,0:T(8,128)(2,1)} %green_ref.3, f32[8,48,640]{2,1,0:T(8,128)} %observed_ref.1, ...), custom_call_target="tpu_custom_call" | custom-call | tf_op jit(solution)/shard_map/forward/pallas_call | solution.py:92
  4.1 0.0 copy-start
  4.1 21.7 %all_to_all.20.parts_ref = bf16[32,64,128]{2,1,0:T(8,128)(2,1)S(1)} all-to-all(bf16[32,64,128]{2,1,0:T(8,128)(2,1)} %get-tuple-element.7), channel_id=1, replica_groups=mesh['z'=16,'x'=4,'c'=2,'y'=4] {'x','c','y'}, dimensions={0} | all-to-all | bytes 1048576 | tf_op jit(solution)/shard_map/all_to_all | solution.py:213
  25.9 0.1 plane_sum.1
  26.0 25.8 %all_to_all.21.parts_ref = bf16[16,64,128]{2,1,0:T(8,128)(2,1)S(1)} all-to-all(bf16[16,64,128]{2,1,0:T(8,128)(2,1)S(1)} %plane_sum.1), channel_id=1, replica_groups=mesh['z'=16,'x'=4,'c'=2,'y'=4] {'z'}, dimensions={0} | all-to-all | bytes 524288 | tf_op jit(solution)/shard_map/all_to_all | solution.py:214
  51.7 0.0 copy-start.1
  51.7 0.8 copy-done.1
  52.5 0.1 weigh.1
  52.6 20.8 %all_to_all.22.weighted_ref = bf16[32,64,128]{2,1,0:T(8,128)(2,1)S(1)} all-to-all(bf16[32,64,128]{2,1,0:T(8,128)(2,1)S(1)} %weigh.1), channel_id=1, replica_groups=mesh['z'=16,'x'=4,'c'=2,'y'=4] {'x','c','y'}, dimensions={0} | all-to-all | bytes 1048576 | tf_op jit(solution)/shard_map/all_to_all | solution.py:217
  73.4 0.0 copy-done.2
  73.4 0.0 copy-done
  73.4 1.9 %adjoint.1 = f32[384,256]{1,0:T(8,128)S(1)} custom-call(s32[1]{0:T(128)} %bitcast.place_ref, s32[31]{0:T(128)S(1)} %copy-done.2, bf16[32,64,128]{2,1,0:T(8,128)(2,1)S(1)} %all_to_all.22.weighted_ref, bf16[8,640,256]{2,1,0:T(8,128)(2,1)S(1)} %copy-done), custom_call_target="tpu_custom_call" | custom-call | tf_op jit(solution)/shard_map/adjoint/pallas_call | solution.py:191
  75.3 9.6 %all_to_all.23 = f32[4,12,8,256]{3,2,1,0:T(8,128)S(1)} all-to-all(f32[4,12,8,256]{3,2,1,0:T(8,128)S(1)} %bitcast.5), channel_id=1, replica_groups=mesh['z'=16,'x'=4,'c'=2,'y'=4] {'y'}, dimensions={0} | all-to-all | bytes 786432 | tf_op jit(solution)/shard_map/all_to_all | solution.py:221
  84.9 0.7 reduce_sum.9
Async XLA Ops:
  0.0 73.4 %copy-start.2 = (s32[31]{0:T(128)S(1)}, s32[31]{0:T(128)}, u32[]{:S(2)}) copy-start(s32[31]{0:T(128)} %gaps_ref.3) | copy-start | bytes 376
  4.1 69.3 %copy-start = (bf16[8,640,256]{2,1,0:T(8,128)(2,1)S(1)}, bf16[8,640,256]{2,1,0:T(8,128)(2,1)}, u32[]{:S(2)}) copy-start(bf16[8,640,256]{2,1,0:T(8,128)(2,1)} %green_ref.3) | copy-start | bytes 7864324
  51.7 0.8 copy-start.1

commit v5 on v4

--- a/solution.py
+++ b/solution.py
@@ -103,8 +103,8 @@
             pltpu.SemaphoreType.DMA((5,)),
         ],
         out_shape=[
-            jax.ShapeDtypeStruct((owners, TALL, WIDE), wire),
-            jax.ShapeDtypeStruct((TALL + 8, WIDE), observed.dtype),
+            pltpu.VMEM((owners, TALL, WIDE), wire),
+            pltpu.VMEM((TALL + 8, WIDE), observed.dtype),
         ],
         name="forward",
     )(place, owner, gaps, source, green, observed, level)
@@ -130,16 +130,13 @@
     )(parts)
 
 
-def weigh_kernel(parts_ref, side_ref, out_ref, side, sem):
-    side_in = pltpu.make_async_copy(side_ref, side, sem)
-    side_in.start()
+def weigh_kernel(parts_ref, side_ref, out_ref):
     value = parts_ref[0].astype(jnp.float32)
     for p in range(1, parts_ref.shape[0]):
         value = value + parts_ref[p].astype(jnp.float32)
-    side_in.wait()
     tall = parts_ref.shape[1]
-    misfit = value - side[pl.ds(0, tall), :]
-    threshold = side[pl.ds(tall, 1), :]
+    misfit = value - side_ref[pl.ds(0, tall), :]
+    threshold = side_ref[pl.ds(tall, 1), :]
     weighted = (misfit * threshold / jnp.maximum(jnp.abs(misfit), threshold)).astype(out_ref.dtype)
     for q in range(out_ref.shape[0]):
         out_ref[q] = weighted
@@ -148,13 +145,30 @@
 def weigh(parts, side, copies):
     return pl.pallas_call(
         weigh_kernel,
-        in_specs=[VMEM, HBM],
-        out_specs=VMEM,
-        scratch_shapes=[pltpu.VMEM(side.shape, side.dtype), pltpu.SemaphoreType.DMA],
+        in_specs=[VMEM, VMEM],
+        out_specs=VMEM,
         out_shape=jax.ShapeDtypeStruct((copies,) + parts.shape[1:], jnp.bfloat16),
         compiler_params=LIMIT,
         name="weigh",
     )(parts, side)
+
+
+def fold_kernel(parts_ref, out_ref):
+    value = parts_ref[0]
+    for y in range(1, parts_ref.shape[0]):
+        value = value + parts_ref[y]
+    out_ref[...] = value
+
+
+def fold(parts):
+    return pl.pallas_call(
+        fold_kernel,
+        in_specs=[VMEM],
+        out_specs=VMEM,
+        out_shape=jax.ShapeDtypeStruct(parts.shape[1:], parts.dtype),
+        compiler_params=LIMIT,
+        name="fold",
+    )(parts)
 
 
 def adjoint_kernel(place_ref, gaps_ref, weighted_ref, green_ref, out_ref, flat, late, *, rows, nb):
@@ -218,7 +232,7 @@
 
     terms = adjoint(place, lag_gaps, weighted, green, rows, steps, 4)
     terms = terms.reshape(groups, steps // groups, rows, cells)
-    terms = jnp.sum(lax.all_to_all(terms, "y", 0, 0, tiled=True), axis=0)
+    terms = fold(lax.all_to_all(terms, "y", 0, 0, tiled=True))
     return terms.transpose(1, 0, 2)
 
 

time: 86 us -> 84 us (0.977)
    all_to_all x1, blocking collectives: 21.7 us -> 20.8 us  [body(): parts = lax.all_to_all(parts, PLANE, 0, 0, tiled=True)]
where the time goes in v5:
time: 84 us; the launch traced here: 83.8 us
  blocking collectives  77.6 us (92%)
  Pallas kernels  6.06 us (7%)
    all_to_all x1, blocking collectives, body(): lax.all_to_all(plane_sum(parts, depth, WIRE), 'z', 0, 0, tiled=True)  26.4 us
    all_to_all x1, blocking collectives, body(): parts = lax.all_to_all(parts, PLANE, 0, 0, tiled=True)  20.8 us
    all_to_all x1, blocking collectives, body(): weighted = lax.all_to_all(weighted, PLANE, 0, 0, tiled=True)  20.8 us
    all_to_all x1, blocking collectives, body(): terms = fold(lax.all_to_all(terms, 'y', 0, 0, tiled=True))  9.58 us
    pallas_call x1, Pallas kernels, forward(): pl.pallas_call(forward_kernel, in_specs=[SMEM, SMEM, HBM, HBM, HBM, HBM,...  3.33 us
    pallas_call x1, Pallas kernels, adjoint(): pl.pallas_call(functools.partial(adjoint_kernel, rows=rows, nb=nb), in_sp...  1.9 us

profile of v5, /device:TPU:1, one launch (start us, length us, event | category | flops | bytes accessed | tf_op | source)
XLA Modules:
  0.0 83.8 jit_solution(5317140120199284769)
XLA Ops:
  0.0 3.3 %forward.1 = (bf16[32,64,128]{2,1,0:T(8,128)(2,1)S(1)}, f32[72,128]{1,0:T(8,128)S(1)}) custom-call(s32[1]{0:T(128)} %bitcast.place_ref, s32[1]{0:T(128)} %bitcast.1.owner_ref, s32[31]{0:T(128)} %gaps_ref.3, bf16[8,48,256]{2,1,0:T(8,128)(2,1)} %source_ref.1, bf16[8,640,256]{2,1,0:T(8,128)(2,1)} %green_ref.3, f32[8,48,640]{2,1,0:T(8,128)} %observed_ref.1, ...), custom_call_target="tpu_custom_call" | custom-call | tf_op jit(solution)/shard_map/forward/pallas_call | solution.py:92
  3.3 0.0 copy-start
  3.3 0.0 copy-start.1
  3.4 20.8 %all_to_all.20.parts_ref = bf16[32,64,128]{2,1,0:T(8,128)(2,1)S(1)} all-to-all(bf16[32,64,128]{2,1,0:T(8,128)(2,1)S(1)} %get-tuple-element.7), channel_id=1, replica_groups=mesh['z'=16,'x'=4,'c'=2,'y'=4] {'x','c','y'}, dimensions={0} | all-to-all | bytes 1048576 | tf_op jit(solution)/shard_map/all_to_all | solution.py:227
  24.2 0.1 plane_sum.1
  24.3 26.4 %all_to_all.21.parts_ref = bf16[16,64,128]{2,1,0:T(8,128)(2,1)S(1)} all-to-all(bf16[16,64,128]{2,1,0:T(8,128)(2,1)S(1)} %plane_sum.1), channel_id=1, replica_groups=mesh['z'=16,'x'=4,'c'=2,'y'=4] {'z'}, dimensions={0} | all-to-all | bytes 524288 | tf_op jit(solution)/shard_map/all_to_all | solution.py:228
  50.7 0.1 weigh.1
  50.8 20.8 %all_to_all.22.weighted_ref = bf16[32,64,128]{2,1,0:T(8,128)(2,1)S(1)} all-to-all(bf16[32,64,128]{2,1,0:T(8,128)(2,1)S(1)} %weigh.1), channel_id=1, replica_groups=mesh['z'=16,'x'=4,'c'=2,'y'=4] {'x','c','y'}, dimensions={0} | all-to-all | bytes 1048576 | tf_op jit(solution)/shard_map/all_to_all | solution.py:231
  71.6 0.0 copy-done
  71.6 0.0 copy-done.1
  71.6 1.9 %adjoint.1 = f32[384,256]{1,0:T(8,128)S(1)} custom-call(s32[1]{0:T(128)} %bitcast.place_ref, s32[31]{0:T(128)S(1)} %copy-done.1, bf16[32,64,128]{2,1,0:T(8,128)(2,1)S(1)} %all_to_all.22.weighted_ref, bf16[8,640,256]{2,1,0:T(8,128)(2,1)S(1)} %copy-done), custom_call_target="tpu_custom_call" | custom-call | tf_op jit(solution)/shard_map/adjoint/pallas_call | solution.py:205
  73.5 9.6 %all_to_all.23.parts_ref = f32[4,12,8,256]{3,2,1,0:T(8,128)S(1)} all-to-all(f32[4,12,8,256]{3,2,1,0:T(8,128)S(1)} %bitcast.5), channel_id=1, replica_groups=mesh['z'=16,'x'=4,'c'=2,'y'=4] {'y'}, dimensions={0} | all-to-all | bytes 786432 | tf_op jit(solution)/shard_map/all_to_all | solution.py:235
  83.1 0.7 fold.1
Async XLA Ops:
  3.3 68.3 %copy-start = (bf16[8,640,256]{2,1,0:T(8,128)(2,1)S(1)}, bf16[8,640,256]{2,1,0:T(8,128)(2,1)}, u32[]{:S(2)}) copy-start(bf16[8,640,256]{2,1,0:T(8,128)(2,1)} %green_ref.3) | copy-start | bytes 7864324
  3.3 68.2 %copy-start.1 = (s32[31]{0:T(128)S(1)}, s32[31]{0:T(128)}, u32[]{:S(2)}) copy-start(s32[31]{0:T(128)} %gaps_ref.3) | copy-start | bytes 376

commit v6 on v5

--- a/solution.py
+++ b/solution.py
@@ -8,7 +8,7 @@
 
 PLANE = ("x", "c", "y")
 TALL, WIDE = 64, 128
-WIRE = jnp.bfloat16
+WIRE = jnp.float32
 VMEM = pl.BlockSpec(memory_space=pltpu.VMEM)
 SMEM = pl.BlockSpec(memory_space=pltpu.SMEM)
 HBM = pl.BlockSpec(memory_space=pl.ANY)

time: 84 us -> 101 us (1.20)
  blocking collectives: 77.6 us -> 93.9 us
    all_to_all x1, blocking collectives: 26.4 us -> 36.6 us  [body(): lax.all_to_all(plane_sum(parts, depth, WIRE), 'z', 0, 0, tiled=True)]
    all_to_all x1, blocking collectives: 20.8 us -> 25.9 us  [body(): parts = lax.all_to_all(parts, PLANE, 0, 0, tiled=True)]
    all_to_all x1, blocking collectives: 20.8 us -> 21.8 us  [body(): weighted = lax.all_to_all(weighted, PLANE, 0, 0, tiled=True)]
where the time goes in v6:
time: 101 us; the launch traced here: 100 us
  blocking collectives  93.9 us (93%)
  Pallas kernels  6.07 us (6%)
    all_to_all x1, blocking collectives, body(): lax.all_to_all(plane_sum(parts, depth, WIRE), 'z', 0, 0, tiled=True)  36.6 us
    all_to_all x1, blocking collectives, body(): parts = lax.all_to_all(parts, PLANE, 0, 0, tiled=True)  25.9 us
    all_to_all x1, blocking collectives, body(): weighted = lax.all_to_all(weighted, PLANE, 0, 0, tiled=True)  21.8 us
    all_to_all x1, blocking collectives, body(): terms = fold(lax.all_to_all(terms, 'y', 0, 0, tiled=True))  9.58 us
    pallas_call x1, Pallas kernels, forward(): pl.pallas_call(forward_kernel, in_specs=[SMEM, SMEM, HBM, HBM, HBM, HBM,...  3.33 us

profile of v6, /device:TPU:1, one launch (start us, length us, event | category | flops | bytes accessed | tf_op | source)
XLA Modules:
  0.0 100.0 jit_solution(10957384059658599343)
XLA Ops:
  0.0 3.3 %forward.1 = (f32[32,64,128]{2,1,0:T(8,128)S(1)}, f32[72,128]{1,0:T(8,128)S(1)}) custom-call(s32[1]{0:T(128)} %bitcast.place_ref, s32[1]{0:T(128)} %bitcast.1.owner_ref, s32[31]{0:T(128)} %gaps_ref.3, bf16[8,48,256]{2,1,0:T(8,128)(2,1)} %source_ref.1, bf16[8,640,256]{2,1,0:T(8,128)(2,1)} %green_ref.3, f32[8,48,640]{2,1,0:T(8,128)} %observed_ref.1, ...), custom_call_target="tpu_custom_call" | custom-call | tf_op jit(solution)/shard_map/forward/pallas_call | solution.py:92
  3.3 25.9 %all_to_all.20.parts_ref = f32[32,64,128]{2,1,0:T(8,128)S(1)} all-to-all(f32[32,64,128]{2,1,0:T(8,128)S(1)} %get-tuple-element.7), channel_id=1, replica_groups=mesh['z'=16,'x'=4,'c'=2,'y'=4] {'x','c','y'}, dimensions={0} | all-to-all | bytes 2097152 | tf_op jit(solution)/shard_map/all_to_all | solution.py:227
  29.2 0.0 copy-start
  29.2 0.0 copy-start.1
  29.2 0.1 plane_sum.1
  29.3 36.6 %all_to_all.21.parts_ref = f32[16,64,128]{2,1,0:T(8,128)S(1)} all-to-all(f32[16,64,128]{2,1,0:T(8,128)S(1)} %plane_sum.1), channel_id=1, replica_groups=mesh['z'=16,'x'=4,'c'=2,'y'=4] {'z'}, dimensions={0} | all-to-all | bytes 1048576 | tf_op jit(solution)/shard_map/all_to_all | solution.py:228
  65.9 0.1 weigh.1
  66.0 21.8 %all_to_all.22.weighted_ref = bf16[32,64,128]{2,1,0:T(8,128)(2,1)S(1)} all-to-all(bf16[32,64,128]{2,1,0:T(8,128)(2,1)S(1)} %weigh.1), channel_id=1, replica_groups=mesh['z'=16,'x'=4,'c'=2,'y'=4] {'x','c','y'}, dimensions={0} | all-to-all | bytes 1048576 | tf_op jit(solution)/shard_map/all_to_all | solution.py:231
  87.9 0.0 copy-done
  87.9 0.0 copy-done.1
  87.9 1.9 %adjoint.1 = f32[384,256]{1,0:T(8,128)S(1)} custom-call(s32[1]{0:T(128)} %bitcast.place_ref, s32[31]{0:T(128)S(1)} %copy-done.1, bf16[32,64,128]{2,1,0:T(8,128)(2,1)S(1)} %all_to_all.22.weighted_ref, bf16[8,640,256]{2,1,0:T(8,128)(2,1)S(1)} %copy-done), custom_call_target="tpu_custom_call" | custom-call | tf_op jit(solution)/shard_map/adjoint/pallas_call | solution.py:205
  89.8 9.6 %all_to_all.23.parts_ref = f32[4,12,8,256]{3,2,1,0:T(8,128)S(1)} all-to-all(f32[4,12,8,256]{3,2,1,0:T(8,128)S(1)} %bitcast.5), channel_id=1, replica_groups=mesh['z'=16,'x'=4,'c'=2,'y'=4] {'y'}, dimensions={0} | all-to-all | bytes 786432 | tf_op jit(solution)/shard_map/all_to_all | solution.py:235
  99.4 0.7 fold.1
Async XLA Ops:
  29.2 58.7 %copy-start = (bf16[8,640,256]{2,1,0:T(8,128)(2,1)S(1)}, bf16[8,640,256]{2,1,0:T(8,128)(2,1)}, u32[]{:S(2)}) copy-start(bf16[8,640,256]{2,1,0:T(8,128)(2,1)} %green_ref.3) | copy-start | bytes 7864324
  29.2 58.7 %copy-start.1 = (s32[31]{0:T(128)S(1)}, s32[31]{0:T(128)}, u32[]{:S(2)}) copy-start(s32[31]{0:T(128)} %gaps_ref.3) | copy-start | bytes 376

commit v7 on v5

--- a/solution.py
+++ b/solution.py
@@ -225,7 +225,10 @@
     level = huber_level.reshape(sensors // WIDE, WIDE)
     parts, side = forward(place, owner, lag_gaps, source, green, observed, level, owners, WIRE)
     parts = lax.all_to_all(parts, PLANE, 0, 0, tiled=True)
-    planes = lax.all_to_all(plane_sum(parts, depth, WIRE), "z", 0, 0, tiled=True)
+    cores = lax.axis_size("c")
+    turned = [[(p + depth // 2) % depth * cores + c for p in range(depth)] for c in range(cores)]
+    planes = plane_sum(parts, depth, WIRE)
+    planes = lax.all_to_all(planes, ("z", "c"), 0, 0, axis_index_groups=turned, tiled=True)
 
     weighted = weigh(planes, side, owners)
     weighted = lax.all_to_all(weighted, PLANE, 0, 0, tiled=True)

time: 84 us -> 81.5 us (0.970)
  blocking collectives: 77.6 us -> 75.1 us
    all_to_all x1, blocking collectives: 20.8 us -> 15.3 us  [body(): weighted = lax.all_to_all(weighted, PLANE, 0, 0, tiled=True)]
    all_to_all x1, blocking collectives: 26.4 us -> 29.4 us  [body(): lax.all_to_all(planes, ('z', 'c'), 0, 0, axis_index_groups=turned, tiled=...]
where the time goes in v7:
time: 81.5 us; the launch traced here: 81.2 us
  blocking collectives  75.1 us (92%)
  Pallas kernels  6.07 us (7%)
    all_to_all x1, blocking collectives, body(): lax.all_to_all(planes, ('z', 'c'), 0, 0, axis_index_groups=turned, tiled=...  29.4 us
    all_to_all x1, blocking collectives, body(): parts = lax.all_to_all(parts, PLANE, 0, 0, tiled=True)  20.8 us
    all_to_all x1, blocking collectives, body(): weighted = lax.all_to_all(weighted, PLANE, 0, 0, tiled=True)  15.3 us
    all_to_all x1, blocking collectives, body(): terms = fold(lax.all_to_all(terms, 'y', 0, 0, tiled=True))  9.57 us
    pallas_call x1, Pallas kernels, forward(): pl.pallas_call(forward_kernel, in_specs=[SMEM, SMEM, HBM, HBM, HBM, HBM,...  3.33 us
    pallas_call x1, Pallas kernels, adjoint(): pl.pallas_call(functools.partial(adjoint_kernel, rows=rows, nb=nb), in_sp...  1.92 us

profile of v7, /device:TPU:1, one launch (start us, length us, event | category | flops | bytes accessed | tf_op | source)
XLA Modules:
  0.0 81.2 jit_solution(1212595592513997933)
XLA Ops:
  0.0 3.3 %forward.1 = (bf16[32,64,128]{2,1,0:T(8,128)(2,1)S(1)}, f32[72,128]{1,0:T(8,128)S(1)}) custom-call(s32[1]{0:T(128)} %bitcast.place_ref, s32[1]{0:T(128)} %bitcast.1.owner_ref, s32[31]{0:T(128)} %gaps_ref.3, bf16[8,48,256]{2,1,0:T(8,128)(2,1)} %source_ref.1, bf16[8,640,256]{2,1,0:T(8,128)(2,1)} %green_ref.3, f32[8,48,640]{2,1,0:T(8,128)} %observed_ref.1, ...), custom_call_target="tpu_custom_call" | custom-call | tf_op jit(solution)/shard_map/forward/pallas_call | solution.py:92
  3.3 0.0 copy-start
  3.3 0.0 copy-start.1
  3.4 20.8 %all_to_all.20.parts_ref = bf16[32,64,128]{2,1,0:T(8,128)(2,1)S(1)} all-to-all(bf16[32,64,128]{2,1,0:T(8,128)(2,1)S(1)} %get-tuple-element.7), channel_id=1, replica_groups=mesh['z'=16,'x'=4,'c'=2,'y'=4] {'x','c','y'}, dimensions={0} | all-to-all | bytes 1048576 | tf_op jit(solution)/shard_map/all_to_all | solution.py:227
  24.2 0.1 plane_sum.1
  24.3 29.4 %all_to_all.21.parts_ref = bf16[16,64,128]{2,1,0:T(8,128)(2,1)S(1)} all-to-all(bf16[16,64,128]{2,1,0:T(8,128)(2,1)S(1)} %plane_sum.1), channel_id=1, replica_groups={{256,288,320,352,384,416,448,480,0,32,64,96,128,160,192,224},{260,292,3..., dimensions={0} | all-to-all | bytes 524288 | tf_op jit(solution)/shard_map/all_to_all | solution.py:231
  53.6 0.1 weigh.1
  53.7 15.3 %all_to_all.22.weighted_ref = bf16[32,64,128]{2,1,0:T(8,128)(2,1)S(1)} all-to-all(bf16[32,64,128]{2,1,0:T(8,128)(2,1)S(1)} %weigh.1), channel_id=1, replica_groups=mesh['z'=16,'x'=4,'c'=2,'y'=4] {'x','c','y'}, dimensions={0} | all-to-all | bytes 1048576 | tf_op jit(solution)/shard_map/all_to_all | solution.py:234
  69.0 0.0 copy-done
  69.0 0.0 copy-done.1
  69.1 1.9 %adjoint.1 = f32[384,256]{1,0:T(8,128)S(1)} custom-call(s32[1]{0:T(128)} %bitcast.place_ref, s32[31]{0:T(128)S(1)} %copy-done.1, bf16[32,64,128]{2,1,0:T(8,128)(2,1)S(1)} %all_to_all.22.weighted_ref, bf16[8,640,256]{2,1,0:T(8,128)(2,1)S(1)} %copy-done), custom_call_target="tpu_custom_call" | custom-call | tf_op jit(solution)/shard_map/adjoint/pallas_call | solution.py:205
  71.0 9.6 %all_to_all.23.parts_ref = f32[4,12,8,256]{3,2,1,0:T(8,128)S(1)} all-to-all(f32[4,12,8,256]{3,2,1,0:T(8,128)S(1)} %bitcast.5), channel_id=1, replica_groups=mesh['z'=16,'x'=4,'c'=2,'y'=4] {'y'}, dimensions={0} | all-to-all | bytes 786432 | tf_op jit(solution)/shard_map/all_to_all | solution.py:238
  80.5 0.7 fold.1
Async XLA Ops:
  3.3 65.7 %copy-start = (bf16[8,640,256]{2,1,0:T(8,128)(2,1)S(1)}, bf16[8,640,256]{2,1,0:T(8,128)(2,1)}, u32[]{:S(2)}) copy-start(bf16[8,640,256]{2,1,0:T(8,128)(2,1)} %green_ref.3) | copy-start | bytes 7864324
  3.3 65.7 %copy-start.1 = (s32[31]{0:T(128)S(1)}, s32[31]{0:T(128)}, u32[]{:S(2)}) copy-start(s32[31]{0:T(128)} %gaps_ref.3) | copy-start | bytes 376

commit v8 on v7

--- a/solution.py
+++ b/solution.py
@@ -226,7 +226,7 @@
     parts, side = forward(place, owner, lag_gaps, source, green, observed, level, owners, WIRE)
     parts = lax.all_to_all(parts, PLANE, 0, 0, tiled=True)
     cores = lax.axis_size("c")
-    turned = [[(p + depth // 2) % depth * cores + c for p in range(depth)] for c in range(cores)]
+    turned = [[(p + depth // 2 + 2 * c) % depth * cores + c for p in range(depth)] for c in range(cores)]
     planes = plane_sum(parts, depth, WIRE)
     planes = lax.all_to_all(planes, ("z", "c"), 0, 0, axis_index_groups=turned, tiled=True)
 

time: 81.5 us -> 81.3 us (level)
    all_to_all x1, blocking collectives: 29.4 us -> 27.8 us  [body(): lax.all_to_all(planes, ('z', 'c'), 0, 0, axis_index_groups=turned, tiled=...]
    all_to_all x1, blocking collectives: 15.3 us -> 16.7 us  [body(): weighted = lax.all_to_all(weighted, PLANE, 0, 0, tiled=True)]
where the time goes in v8:
time: 81.3 us; the launch traced here: 81 us
  blocking collectives  74.9 us (92%)
  Pallas kernels  6.08 us (7%)
    all_to_all x1, blocking collectives, body(): lax.all_to_all(planes, ('z', 'c'), 0, 0, axis_index_groups=turned, tiled=...  27.8 us
    all_to_all x1, blocking collectives, body(): parts = lax.all_to_all(parts, PLANE, 0, 0, tiled=True)  20.8 us
    all_to_all x1, blocking collectives, body(): weighted = lax.all_to_all(weighted, PLANE, 0, 0, tiled=True)  16.7 us
    all_to_all x1, blocking collectives, body(): terms = fold(lax.all_to_all(terms, 'y', 0, 0, tiled=True))  9.57 us
    pallas_call x1, Pallas kernels, forward(): pl.pallas_call(forward_kernel, in_specs=[SMEM, SMEM, HBM, HBM, HBM, HBM,...  3.33 us
    pallas_call x1, Pallas kernels, adjoint(): pl.pallas_call(functools.partial(adjoint_kernel, rows=rows, nb=nb), in_sp...  1.92 us

profile of v8, /device:TPU:1, one launch (start us, length us, event | category | flops | bytes accessed | tf_op | source)
XLA Modules:
  0.0 81.0 jit_solution(1710700508371290797)
XLA Ops:
  0.0 3.3 %forward.1 = (bf16[32,64,128]{2,1,0:T(8,128)(2,1)S(1)}, f32[72,128]{1,0:T(8,128)S(1)}) custom-call(s32[1]{0:T(128)} %bitcast.place_ref, s32[1]{0:T(128)} %bitcast.1.owner_ref, s32[31]{0:T(128)} %gaps_ref.3, bf16[8,48,256]{2,1,0:T(8,128)(2,1)} %source_ref.1, bf16[8,640,256]{2,1,0:T(8,128)(2,1)} %green_ref.3, f32[8,48,640]{2,1,0:T(8,128)} %observed_ref.1, ...), custom_call_target="tpu_custom_call" | custom-call | tf_op jit(solution)/shard_map/forward/pallas_call | solution.py:92
  3.3 0.0 copy-start
  3.3 0.0 copy-start.1
  3.4 20.8 %all_to_all.20.parts_ref = bf16[32,64,128]{2,1,0:T(8,128)(2,1)S(1)} all-to-all(bf16[32,64,128]{2,1,0:T(8,128)(2,1)S(1)} %get-tuple-element.7), channel_id=1, replica_groups=mesh['z'=16,'x'=4,'c'=2,'y'=4] {'x','c','y'}, dimensions={0} | all-to-all | bytes 1048576 | tf_op jit(solution)/shard_map/all_to_all | solution.py:227
  24.2 0.1 plane_sum.1
  24.3 27.8 %all_to_all.21.parts_ref = bf16[16,64,128]{2,1,0:T(8,128)(2,1)S(1)} all-to-all(bf16[16,64,128]{2,1,0:T(8,128)(2,1)S(1)} %plane_sum.1), channel_id=1, replica_groups={{256,288,320,352,384,416,448,480,0,32,64,96,128,160,192,224},{324,356,3..., dimensions={0} | all-to-all | bytes 524288 | tf_op jit(solution)/shard_map/all_to_all | solution.py:231
  52.1 0.1 weigh.1
  52.2 16.7 %all_to_all.22.weighted_ref = bf16[32,64,128]{2,1,0:T(8,128)(2,1)S(1)} all-to-all(bf16[32,64,128]{2,1,0:T(8,128)(2,1)S(1)} %weigh.1), channel_id=1, replica_groups=mesh['z'=16,'x'=4,'c'=2,'y'=4] {'x','c','y'}, dimensions={0} | all-to-all | bytes 1048576 | tf_op jit(solution)/shard_map/all_to_all | solution.py:234
  68.9 0.0 copy-done
  68.9 0.0 copy-done.1
  68.9 1.9 %adjoint.1 = f32[384,256]{1,0:T(8,128)S(1)} custom-call(s32[1]{0:T(128)} %bitcast.place_ref, s32[31]{0:T(128)S(1)} %copy-done.1, bf16[32,64,128]{2,1,0:T(8,128)(2,1)S(1)} %all_to_all.22.weighted_ref, bf16[8,640,256]{2,1,0:T(8,128)(2,1)S(1)} %copy-done), custom_call_target="tpu_custom_call" | custom-call | tf_op jit(solution)/shard_map/adjoint/pallas_call | solution.py:205
  70.8 9.6 %all_to_all.23.parts_ref = f32[4,12,8,256]{3,2,1,0:T(8,128)S(1)} all-to-all(f32[4,12,8,256]{3,2,1,0:T(8,128)S(1)} %bitcast.5), channel_id=1, replica_groups=mesh['z'=16,'x'=4,'c'=2,'y'=4] {'y'}, dimensions={0} | all-to-all | bytes 786432 | tf_op jit(solution)/shard_map/all_to_all | solution.py:238
  80.4 0.7 fold.1
Async XLA Ops:
  3.3 65.5 %copy-start = (bf16[8,640,256]{2,1,0:T(8,128)(2,1)S(1)}, bf16[8,640,256]{2,1,0:T(8,128)(2,1)}, u32[]{:S(2)}) copy-start(bf16[8,640,256]{2,1,0:T(8,128)(2,1)} %green_ref.3) | copy-start | bytes 7864324
  3.3 65.5 %copy-start.1 = (s32[31]{0:T(128)S(1)}, s32[31]{0:T(128)}, u32[]{:S(2)}) copy-start(s32[31]{0:T(128)} %gaps_ref.3) | copy-start | bytes 376
